TPU v7x, 256 devices: a whole 4x4x8 slice. The times are simulated.
256 devices in a mesh: dp: 16 (over z, core), expert: 16 (over x, y).
Axes of the slice: x: 4, y: 4, z: 8, core: 2. Of those that a mesh axis runs over, the one named last changes fastest.
Arguments:
- tokens: bfloat16 [4096, 16, 1536], P('dp', 'expert'), may hold values from -6 to 6
- route_ids: int32 [16, 4096, 2], P('expert', 'dp'), may hold values from 0 to 15, all different within a row; in each aligned block of 256 rows (0 to 255, 256 to 511, ..., all dimensions but the last counted through in order) at most 48 rows name the same one
- router: bfloat16 [16, 1536, 16], P('expert'), may hold values from -0.15625 to 0.15625
- norm_gain: float32 [16, 1536], P('expert'), may hold values from 0.5 to 1.5
- w_in: bfloat16 [16, 16, 1536, 768], P('expert', 'dp'), may hold values from -0.15625 to 0.15625
- w_out: bfloat16 [16, 16, 768, 1536], P('expert', 'dp'), may hold values from -0.21875 to 0.21875
- cotangent: bfloat16 [4096, 16, 1536], P('dp', 'expert'), may hold values from -6 to 6
Outputs:
- normed_out: bfloat16 [4096, 16, 1536], P('dp', 'expert')
- grad_tokens: bfloat16 [4096, 16, 1536], P('dp', 'expert')
- grad_router: float32 [16, 1536, 16], P('expert')
- grad_gain: float32 [16, 1536], P('expert')
- grad_w_in: bfloat16 [16, 16, 1536, 768], P('expert', 'dp')
- grad_w_out: bfloat16 [16, 16, 768, 1536], P('expert', 'dp')
Inputs may be any that keep to these rules, and one draw needn't show every extreme that they name: `route_ids`: the two ids of a row differ. Among the rows of one device (one mixed token, 256 samples, two choices each) no expert is named more than 48 times.
All inputs are finite; a program needn't handle non-finite values.
Results may differ from a plain program's by a relative error of at most 0.015.
Values may be sent and summed in bfloat16 or wider, within the bound.
A program may use at most 64 MiB of HBM per device.

v0:
```python
import jax
import jax.numpy as jnp
from jax import lax
from jax.sharding import PartitionSpec as P

gelu_coef = 0.7978845608028654
cubic_coef = 0.044715
norm_eps = 1e-05


def gathered_total(value, axis):
    return lax.all_gather(value, axis).astype(jnp.float32).sum(0)


def gelu_tanh(value):
    inner = gelu_coef * (value + cubic_coef * value * value * value)
    return 0.5 * value * (1.0 + jnp.tanh(inner))


def gelu_slope(value):
    inner = gelu_coef * (value + cubic_coef * value * value * value)
    tangent = jnp.tanh(inner)
    return 0.5 * (1.0 + tangent) + 0.5 * value * (1.0 - tangent * tangent) * gelu_coef * (
        1.0 + 3.0 * cubic_coef * value * value
    )


def send_back(result):
    return lax.all_to_all(result, "dp", split_axis=0, concat_axis=0, tiled=True)


def pick_rows(hot, rows):
    return lax.dot_general(hot, rows, (((0,), (0,)), ((), ())), preferred_element_type=jnp.float32)


def body(tokens, route_ids, router, norm_gain, w_in, w_out, cotangent):
    row_count = tokens.shape[0]
    model_width = tokens.shape[2]
    experts = lax.axis_size("dp")
    slot_depth = 3 * row_count // experts
    slot_rows = experts * slot_depth
    weight_in = w_in[0, 0]
    weight_out = w_out[0, 0]
    hidden = weight_in.shape[1]
    router_row = router[0]
    gain_row = norm_gain[0]
    own_rows = tokens.reshape(row_count, model_width)
    mixed_rows = lax.all_to_all(own_rows, "expert", split_axis=1, concat_axis=1, tiled=True)
    route_rows = route_ids.reshape(row_count, 2)
    labels = lax.broadcasted_iota(jnp.int32, (row_count, 2, experts), 2)
    chosen = (route_rows[:, :, None] == labels).astype(jnp.int32)
    flat_hot = chosen.reshape(row_count * 2, experts)
    before = jnp.cumsum(flat_hot, axis=0, dtype=jnp.int32) - flat_hot
    slot_place = jnp.sum(before * flat_hot, axis=1, dtype=jnp.int32).reshape(row_count, 2)
    target = route_rows * slot_depth + slot_place
    slot_index = lax.broadcasted_iota(jnp.int32, (slot_rows, row_count), 0)
    first_pick = target[None, :, 0] == slot_index
    second_pick = target[None, :, 1] == slot_index
    placer = jnp.logical_or(first_pick, second_pick).astype(jnp.bfloat16)
    first_hot = first_pick.astype(jnp.bfloat16)
    second_hot = second_pick.astype(jnp.bfloat16)
    chosen_f = chosen.astype(jnp.float32)
    logits = jnp.dot(mixed_rows, router_row, preferred_element_type=jnp.float32)
    picked = jnp.sum(logits[:, None, :] * chosen_f, axis=2)
    gate_value = jax.nn.sigmoid(picked)
    outgoing = jnp.dot(placer, mixed_rows, preferred_element_type=jnp.float32).astype(jnp.bfloat16)
    outgoing = outgoing.reshape(experts, slot_depth, model_width)
    received = lax.all_to_all(outgoing, "dp", split_axis=0, concat_axis=0, tiled=True)
    item_count = received.shape[1]
    expert_input = received.reshape(experts * item_count, model_width)
    pre_act = jnp.dot(expert_input, weight_in, preferred_element_type=jnp.float32)
    act_values = gelu_tanh(pre_act).astype(jnp.bfloat16)
    pre_act, act_values = (pre_act, act_values)
    result = jnp.dot(act_values, weight_out, preferred_element_type=jnp.float32).astype(
        jnp.bfloat16
    )
    sent_back = send_back(result.reshape(experts, item_count, model_width))
    mapped = (
        sent_back,
        pre_act.reshape(experts, item_count, hidden),
        act_values.reshape(experts, item_count, hidden),
        received,
    )
    returned, pre_kept, act_kept, arrived = mapped
    returned_rows = returned.reshape(slot_rows, model_width)
    first_out = pick_rows(first_hot, returned_rows)
    second_out = pick_rows(second_hot, returned_rows)
    expert_sum = gate_value[:, 0:1] * first_out + gate_value[:, 1:2] * second_out
    residual = mixed_rows.astype(jnp.float32) + expert_sum
    row_mean = jnp.mean(residual, axis=1, keepdims=True)
    centered = residual - row_mean
    row_var = jnp.mean(centered * centered, axis=1, keepdims=True)
    inv_std = lax.rsqrt(row_var + norm_eps)
    normed = centered * inv_std
    normed_out = (normed * gain_row[None, :]).astype(jnp.bfloat16)
    cot_f = cotangent.reshape(row_count, model_width).astype(jnp.float32)
    grad_gain = jnp.sum(cot_f * normed, axis=0)
    grad_normed = cot_f * gain_row[None, :]
    grad_resid = inv_std * (
        grad_normed
        - jnp.mean(grad_normed, axis=1, keepdims=True)
        - normed * jnp.mean(grad_normed * normed, axis=1, keepdims=True)
    )
    grad_rounded = grad_resid.astype(jnp.bfloat16)
    first_grad = jnp.sum(grad_resid * first_out, axis=1)
    second_grad = jnp.sum(grad_resid * second_out, axis=1)
    grad_gate = jnp.stack([first_grad, second_grad], axis=1)
    grad_logit = grad_gate * gate_value * (1.0 - gate_value)
    route_grad = jnp.sum(grad_logit[:, :, None] * chosen_f, axis=1)
    selected = jnp.dot(placer, grad_rounded, preferred_element_type=jnp.float32)
    slot_gate = jnp.sum(
        jnp.where(first_pick, gate_value[None, :, 0], 0.0)
        + jnp.where(second_pick, gate_value[None, :, 1], 0.0),
        axis=1,
    )
    grad_send = (
        (slot_gate[:, None] * selected)
        .astype(jnp.bfloat16)
        .reshape(experts, slot_depth, model_width)
    )
    grad_arrived = lax.all_to_all(grad_send, "dp", split_axis=0, concat_axis=0, tiled=True)
    input_rows = arrived.reshape(slot_rows, model_width)
    pre_rows = pre_kept.reshape(slot_rows, hidden)
    act_rows = act_kept.reshape(slot_rows, hidden)
    grad_out_rows = grad_arrived.reshape(slot_rows, model_width)
    grad_act = lax.dot_general(
        grad_out_rows, weight_out, (((1,), (1,)), ((), ())), preferred_element_type=jnp.float32
    )
    grad_pre = (grad_act * gelu_slope(pre_rows)).astype(jnp.bfloat16)
    grad_w_out = pick_rows(act_rows, grad_out_rows).astype(jnp.bfloat16)
    grad_w_in = pick_rows(input_rows, grad_pre).astype(jnp.bfloat16)
    grad_input = lax.dot_general(
        grad_pre, weight_in, (((1,), (1,)), ((), ())), preferred_element_type=jnp.float32
    ).astype(jnp.bfloat16)
    grad_back = lax.all_to_all(
        grad_input.reshape(experts, slot_depth, model_width),
        "dp",
        split_axis=0,
        concat_axis=0,
        tiled=True,
    )
    grad_back_rows = grad_back.reshape(slot_rows, model_width)
    first_input = pick_rows(first_hot, grad_back_rows)
    second_input = pick_rows(second_hot, grad_back_rows)
    router_f = router_row.astype(jnp.float32)
    grad_mixed = (
        grad_resid
        + first_input
        + second_input
        + jnp.dot(route_grad, router_f.T, precision=lax.Precision.HIGHEST)
    )
    router_part = jnp.dot(
        mixed_rows.astype(jnp.float32).T, route_grad, precision=lax.Precision.HIGHEST
    )
    grad_router, grad_gain_sum = (
        gathered_total(router_part.astype(jnp.bfloat16), "dp").astype(jnp.float32),
        gathered_total(grad_gain.astype(jnp.bfloat16), "dp").astype(jnp.float32),
    )
    grad_tokens = lax.all_to_all(
        grad_mixed.astype(jnp.bfloat16), "expert", split_axis=1, concat_axis=1, tiled=True
    )
    return (
        normed_out.reshape(row_count, 1, model_width),
        grad_tokens.reshape(row_count, 1, model_width),
        grad_router.reshape(1, model_width, experts),
        grad_gain_sum.reshape(1, model_width),
        grad_w_in.reshape(1, 1, model_width, hidden),
        grad_w_out.reshape(1, 1, hidden, model_width),
    )


def solution(mesh):
    return jax.shard_map(
        body,
        mesh=mesh,
        in_specs=(
            P("dp", "expert", None),
            P("expert", "dp", None),
            P("expert", None, None),
            P("expert", None),
            P("expert", "dp", None, None),
            P("expert", "dp", None, None),
            P("dp", "expert", None),
        ),
        out_specs=(
            P("dp", "expert", None),
            P("dp", "expert", None),
            P("expert", None, None),
            P("expert", None),
            P("expert", "dp", None, None),
            P("expert", "dp", None, None),
        ),
        check_vma=False,
    )
```

profile of v0, /device:TPU:1, one launch (start us, length us, event | category | flops | bytes accessed | tf_op | source)
XLA Modules:
  0.0 349.8 jit_solution(2821606147934877769)
XLA Ops:
  0.6 0.0 copy-start
  0.6 0.0 copy-start.9
  0.7 2.4 copy.45
  3.1 7.6 %all-to-all-start = ((bf16[256,16,96]{0,2,1:T(8,128)(2,1)}), bf16[256,16,96]{0,2,1:T(8,128)(2,1)S(1)}, u32[]{:S(2)}, u32[]{:S(2)}) async-start(bf16[256,16,96]{0,2,1:T(8,128)(2,1)} %bitcast.98), calls=%async_computation | async-start | bytes 1572864 | tf_op jit(solution)/shard_map/all_to_all | solution.py:48
  10.7 0.0 copy-done.9
  10.7 0.1 copy.47
  10.8 0.1 eq.51
  11.0 0.1 eq.48
  11.1 1.2 reduce-window.6
  12.3 0.2 slice_reduce_fusion.2
  12.6 0.1 fusion.46
  12.7 0.1 reshape.148
  12.8 0.2 slice_reduce_fusion.1
  13.0 10.4 %all-to-all-done = bf16[256,16,96]{0,2,1:T(8,128)(2,1)S(1)} async-done(((bf16[256,16,96]{0,2,1:T(8,128)(2,1)}), bf16[256,16,96]{0,2,1:T(8,128)(2,1)S(1)}, u32[]{:S(2)}, u32[]{:S(2)}) %all-to-all-start) | async-done | bytes 786464 | tf_op jit(solution)/shard_map/all_to_all | solution.py:48
  23.5 0.8 convolution_convert_fusion.4
  24.3 0.0 copy-start.10
  24.3 67.6 %all_to_all.41 = bf16[16,48,1536]{2,1,0:T(8,128)(2,1)S(1)} all-to-all(bf16[16,48,1536]{2,1,0:T(8,128)(2,1)S(1)} %bitcast.95), channel_id=1, replica_groups=mesh['dp'=16,'expert'=16] {'dp'}, dimensions={0} | all-to-all | bytes 4718592 | tf_op jit(solution)/shard_map/all_to_all | solution.py:68
  91.9 1.4 copy-done.4
  93.3 0.0 copy-done.10
  93.3 2.0 fusion.14
  95.3 0.0 copy-done
  95.3 0.0 copy-start.12
  95.3 3.5 %convolution_convert_fusion.3 = bf16[768,1536]{1,0:T(8,128)(2,1)} fusion(bf16[1,1,768,1536]{3,2,1,0:T(8,128)(2,1)S(1)} %copy-done, f32[768,768]{1,0:T(8,128)S(1)} %fusion.14), kind=kOutput, calls=%fused_computation.6 | convolution fusion | flops 1818427392 | bytes 7077888 | tf_op jit(solution)/shard_map/dot_general | solution.py:74
  98.8 0.0 copy-done.12
  98.8 4.5 %all-to-all-start.2 = ((bf16[16,48,1536]{2,1,0:T(8,128)(2,1)}), bf16[16,48,1536]{2,1,0:T(8,128)(2,1)}, u32[]{:S(2)}, u32[]{:S(2)}) async-start(bf16[16,48,1536]{2,1,0:T(8,128)(2,1)} %bitcast.106), calls=%async_computation.2 | async-start | bytes 4718592 | tf_op jit(solution)/shard_map/all_to_all | solution.py:29
  103.3 0.1 copy.48
  103.4 0.0 copy-done.8
  103.5 1.2 copy.46
  104.6 0.2 fusion.42
  104.9 0.2 add_reduce_fusion
  105.1 51.9 %all-to-all-done.2 = bf16[16,48,1536]{2,1,0:T(8,128)(2,1)} async-done(((bf16[16,48,1536]{2,1,0:T(8,128)(2,1)}), bf16[16,48,1536]{2,1,0:T(8,128)(2,1)}, u32[]{:S(2)}, u32[]{:S(2)}) %all-to-all-start.2) | async-done | bytes 2359328 | tf_op jit(solution)/shard_map/all_to_all | solution.py:29
  157.0 2.6 fusion.30
  159.6 0.0 copy-done.2
  159.6 0.0 copy-start.3
  159.6 2.8 fusion.50
  162.4 0.3 multiply_reduce_fusion.2
  162.7 0.7 fusion.23
  163.4 1.7 multiply_reduce_fusion.1
  165.1 0.8 multiply_convert_fusion
  165.9 0.0 copy-start.13
  165.9 62.0 %all_to_all.42 = bf16[16,48,1536]{2,1,0:T(8,128)(2,1)S(1)} all-to-all(bf16[16,48,1536]{2,1,0:T(8,128)(2,1)S(1)} %bitcast.94), channel_id=1, replica_groups=mesh['dp'=16,'expert'=16] {'dp'}, dimensions={0} | all-to-all | bytes 4718592 | tf_op jit(solution)/shard_map/all_to_all | solution.py:121
  227.9 2.9 fusion.9
  230.9 3.4 convolution_convert_fusion.2
  234.3 0.0 copy-done.15
  234.3 4.3 %all-to-all-start.4 = ((bf16[16,48,1536]{2,1,0:T(8,128)(2,1)}), bf16[16,48,1536]{2,1,0:T(8,128)(2,1)}, u32[]{:S(2)}, u32[]{:S(2)}) async-start(bf16[16,48,1536]{2,1,0:T(8,128)(2,1)} %bitcast.105), calls=%async_computation.4 | async-start | bytes 4718592 | tf_op jit(solution)/shard_map/all_to_all | solution.py:135
  238.7 64.8 %all-gather.2 = bf16[16,1,1536]{2,1,0:T(2,128)(2,1)S(1)} all-gather(bf16[1,1,1536]{2,1,0:T(2,128)(2,1)S(1)} %reshape.168), channel_id=3, replica_groups=mesh['dp'=16,'expert'=16] {'dp'}, dimensions={0}, use_global_device_ids=true | all-gather | bytes 52224 | tf_op jit(solution)/shard_map/all_gather | solution.py:12
  303.4 0.1 convert_reduce_fusion
  303.6 0.6 reshape.160
  304.2 0.7 fusion.16
  304.9 16.9 %all-gather = bf16[24576,16]{0,1:T(8,128)(2,1)S(1)} all-gather(bf16[1536,16]{0,1:T(8,128)(2,1)S(1)} %fusion.16), channel_id=2, replica_groups=mesh['dp'=16,'expert'=16] {'dp'}, dimensions={0}, use_global_device_ids=true | all-gather | bytes 835584 | tf_op jit(solution)/shard_map/all_gather | solution.py:12
  321.8 0.1 convert_element_type.110
  321.9 0.9 copy.55
  322.8 0.9 bitcast_reduce_fusion
  323.7 0.0 all-to-all-done.4
  323.7 2.9 convolution_add_fusion.2
  326.6 2.5 convolution_add_fusion.1
  329.1 0.9 fusion.2
  330.0 1.2 copy.52
  331.2 3.8 %all-to-all-start.5 = ((bf16[256,16,96]{0,2,1:T(8,128)(2,1)}), bf16[256,16,96]{0,2,1:T(8,128)(2,1)S(1)}, u32[]{:S(2)}, u32[]{:S(2)}) async-start(bf16[256,16,96]{0,2,1:T(8,128)(2,1)} %bitcast.100), calls=%async_computation.5 | async-start | bytes 1572864 | tf_op jit(solution)/shard_map/all_to_all | solution.py:159
  335.0 5.6 %fusion = bf16[1,1,1536,768]{3,2,1,0:T(8,128)(2,1)} fusion(bf16[768,1536]{1,0:T(8,128)(2,1)} %bitcast.102, bf16[768,768]{1,0:T(8,128)(2,1)} %copy-done.15), kind=kOutput, calls=%fused_computation.8 | convolution fusion | flops 1813118976 | bytes 5898240 | tf_op jit(solution)/shard_map/dot_general | solution.py:33
  340.6 0.0 copy-done.6
  340.6 3.6 %fusion.1 = bf16[1,1,768,1536]{3,2,1,0:T(8,128)(2,1)} fusion(bf16[768,1536]{1,0:T(8,128)(2,1)S(1)} %bitcast.104, f32[768,768]{1,0:T(8,128)S(1)} %copy-done.14), kind=kOutput, calls=%fused_computation.9 | convolution fusion | flops 1818427392 | bytes 7077888 | tf_op jit(solution)/shard_map/dot_general | solution.py:33
  344.2 4.5 %all-to-all-done.5 = bf16[256,16,96]{0,2,1:T(8,128)(2,1)S(1)} async-done(((bf16[256,16,96]{0,2,1:T(8,128)(2,1)}), bf16[256,16,96]{0,2,1:T(8,128)(2,1)S(1)}, u32[]{:S(2)}, u32[]{:S(2)}) %all-to-all-start.5) | async-done | bytes 786464 | tf_op jit(solution)/shard_map/all_to_all | solution.py:159
  348.7 1.2 copy.53
  (31 shorter events, 0.2 us)
Async XLA Ops:
  0.6 94.6 %copy-start = (bf16[1,1,768,1536]{3,2,1,0:T(8,128)(2,1)S(1)}, bf16[1,1,768,1536]{3,2,1,0:T(8,128)(2,1)}, u32[]{:S(2)}) copy-start(bf16[1,1,768,1536]{3,2,1,0:T(8,128)(2,1)} %param.12) | copy-start | bytes 7077892
  0.6 10.0 %copy-start.9 = (s32[1,256,2]{1,2,0:T(2,128)S(1)}, s32[1,256,2]{1,2,0:T(2,128)}, u32[]{:S(2)}) copy-start(s32[1,256,2]{1,2,0:T(2,128)} %param.8) | copy-start | bytes 6148
  3.1 20.4 %all-to-all-start = ((bf16[256,16,96]{0,2,1:T(8,128)(2,1)}), bf16[256,16,96]{0,2,1:T(8,128)(2,1)S(1)}, u32[]{:S(2)}, u32[]{:S(2)}) async-start(bf16[256,16,96]{0,2,1:T(8,128)(2,1)} %bitcast.98), calls=%async_computation | async-start | bytes 1572864 | tf_op jit(solution)/shard_map/all_to_all | solution.py:48
  24.3 69.0 %copy-start.10 = (bf16[1,1,1536,768]{3,2,1,0:T(8,128)(2,1)S(1)}, bf16[1,1,1536,768]{3,2,1,0:T(8,128)(2,1)}, u32[]{:S(2)}) copy-start(bf16[1,1,1536,768]{3,2,1,0:T(8,128)(2,1)} %param.11) | copy-start | bytes 7077892
  91.9 1.4 copy-start.4
  95.3 3.6 %copy-start.12 = (f32[768,768]{1,0:T(8,128)}, f32[768,768]{1,0:T(8,128)S(1)}, u32[]{:S(2)}) copy-start(f32[768,768]{1,0:T(8,128)S(1)} %fusion.14) | copy-start | bytes 7077892
  98.8 4.6 %copy-start.8 = (f32[1,1536]{1,0:T(1,128)S(1)}, f32[1,1536]{1,0:T(1,128)}, u32[]{:S(2)}) copy-start(f32[1,1536]{1,0:T(1,128)} %param.10) | copy-start | bytes 18436
  98.8 5.8 %copy-start.7 = (bf16[1,1536,16]{1,2,0:T(8,128)(2,1)S(1)}, bf16[1,1536,16]{1,2,0:T(8,128)(2,1)}, u32[]{:S(2)}) copy-start(bf16[1,1536,16]{1,2,0:T(8,128)(2,1)} %param.9) | copy-start | bytes 147460
  98.8 58.2 %all-to-all-start.2 = ((bf16[16,48,1536]{2,1,0:T(8,128)(2,1)}), bf16[16,48,1536]{2,1,0:T(8,128)(2,1)}, u32[]{:S(2)}, u32[]{:S(2)}) async-start(bf16[16,48,1536]{2,1,0:T(8,128)(2,1)} %bitcast.106), calls=%async_computation.2 | async-start | bytes 4718592 | tf_op jit(solution)/shard_map/all_to_all | solution.py:29
  157.0 2.6 copy-start.2
  159.6 3.1 copy-start.3
  165.1 62.8 %copy-start.1 = (f32[256,1536]{1,0:T(8,128)}, f32[256,1536]{1,0:T(8,128)S(1)}, u32[]{:S(2)}) copy-start(f32[256,1536]{1,0:T(8,128)S(1)} %get-tuple-element.37) | copy-start | bytes 4718596
  165.9 62.0 %copy-start.13 = (f32[768,768]{1,0:T(8,128)S(1)}, f32[768,768]{1,0:T(8,128)}, u32[]{:S(2)}) copy-start(f32[768,768]{1,0:T(8,128)} %copy-done.12) | copy-start | bytes 7077892
  227.9 2.9 copy-start.5
  227.9 2.9 copy-start.11
  230.8 3.4 copy-start.15
  234.3 89.4 %all-to-all-start.4 = ((bf16[16,48,1536]{2,1,0:T(8,128)(2,1)}), bf16[16,48,1536]{2,1,0:T(8,128)(2,1)}, u32[]{:S(2)}, u32[]{:S(2)}) async-start(bf16[16,48,1536]{2,1,0:T(8,128)(2,1)} %bitcast.105), calls=%async_computation.4 | async-start | bytes 4718592 | tf_op jit(solution)/shard_map/all_to_all | solution.py:135
  331.2 17.5 %all-to-all-start.5 = ((bf16[256,16,96]{0,2,1:T(8,128)(2,1)}), bf16[256,16,96]{0,2,1:T(8,128)(2,1)S(1)}, u32[]{:S(2)}, u32[]{:S(2)}) async-start(bf16[256,16,96]{0,2,1:T(8,128)(2,1)} %bitcast.100), calls=%async_computation.5 | async-start | bytes 1572864 | tf_op jit(solution)/shard_map/all_to_all | solution.py:159
  335.0 5.6 %copy-start.6 = (bf16[16,48,1536]{2,1,0:T(8,128)(2,1)S(1)}, bf16[16,48,1536]{2,1,0:T(8,128)(2,1)}, u32[]{:S(2)}) copy-start(bf16[16,48,1536]{2,1,0:T(8,128)(2,1)} %copy-done.5) | copy-start | bytes 7077892
  335.0 5.6 %copy-start.14 = (f32[768,768]{1,0:T(8,128)S(1)}, f32[768,768]{1,0:T(8,128)}, u32[]{:S(2)}) copy-start(f32[768,768]{1,0:T(8,128)} %copy-done.12) | copy-start | bytes 7077892
where the time goes:
time: 350 us
  blocking collectives  211 us (60%)
  waiting for transfers between devices  66.9 us (19%)
  matrix products  35.2 us (10%)
  starting transfers between devices  20.2 us (6%)
  local copies, waits for them, and re-layouts  9.95 us (3%)
  other arithmetic  5.39 us (2%)
    all_gather x2, blocking collectives, gathered_total(): return lax.all_gather(value, axis).astype(jnp.float32).sum(0)  81.6 us
    all_to_all x1, blocking collectives, body(): lax.all_to_all(outgoing, 'dp', split_axis=0, concat_axis=0, tiled=True)  67.6 us
    all_to_all x1, blocking collectives, body(): lax.all_to_all(grad_send, 'dp', split_axis=0, concat_axis=0, tiled=True)  62 us
    all_to_all x1, waiting for transfers between devices, send_back(): return lax.all_to_all(result, 'dp', split_axis=0, concat_axis=0, tiled=True)  51.9 us
    dot_general x6, matrix products, pick_rows(): lax.dot_general(hot, rows, (((0,), (0,)), ((), ())), preferred_element_ty...  19.9 us
    all_to_all x1, waiting for transfers between devices, body(): lax.all_to_all(own_rows, 'expert', split_axis=1, concat_axis=1, tiled=True)  10.4 us
    all_to_all x1, starting transfers between devices, body(): lax.all_to_all(own_rows, 'expert', split_axis=1, concat_axis=1, tiled=True)  7.58 us
  transfers between devices with their start and end apart: 4, of which 3 were waited for; matrix products, arithmetic and copies ran while one was open for 5% of the time, Pallas kernels for 0%

commit v1 on v0

v1 whole, which is shorter than its diff:
```python
import functools

import jax
import jax.numpy as jnp
from jax import lax
from jax.experimental import pallas as pl
from jax.experimental.pallas import tpu as pltpu
from jax.sharding import PartitionSpec as P

MESH = pl.DeviceIdType.MESH
F32 = jnp.float32
BF16 = jnp.bfloat16

gelu_coef = 0.7978845608028654
cubic_coef = 0.044715
norm_eps = 1e-05

N = 16
NC = 4
NG = 4
RING = 8
STEPS = (0, 1, -1, 2, -2, 3, -3, 4)
BACK = (0, 2, 1, 4, 3, 6, 5, 7)
TILE = 32


def inverse(r):
    return 2 * BACK[r // 2] + r % 2


def dot(a, b):
    return lax.dot_general(a, b, (((1,), (0,)), ((), ())), preferred_element_type=F32)


def dot_nt(a, b):
    return lax.dot_general(a, b, (((1,), (1,)), ((), ())), preferred_element_type=F32)


def dot_tn(a, b):
    return lax.dot_general(a, b, (((0,), (0,)), ((), ())), preferred_element_type=F32)


def gelu_and_slope(value):
    inner = gelu_coef * (value + cubic_coef * value * value * value)
    tangent = jnp.tanh(inner)
    half = 0.5 * (1.0 + tangent)
    slope = half + 0.5 * value * (1.0 - tangent * tangent) * gelu_coef * (
        1.0 + 3.0 * cubic_coef * value * value
    )
    return value * half, slope


def kernel(
    tok_h, ids_ref, rt_ref, gain_ref, win_h, wout_h, cot_h,
    no_h, gt_h, gr_ref, gg_ref, gwi_h, gwo_h,
    tok, tok_t, mix_t, mixed, cot, win, wout, rt4, place_m, place_t,
    xs, xr, pre, logit, gate, act, ys, yr, acc, grd, gs, gr, gp, dos, ds, dr,
    norm_o, gwi, gwo, gm_t, gt_t, gt_o, ggp, rcol, small,
    gain_s, gain_r, col_s, col_r,
    load_sem, mix_ss, mix_rs, a_ss, a_rs, b_ss, b_rs, c_ss, c_rs, d_ss, d_rs,
    e_ss, e_rs, gn_ss, gn_rs, cl_ss, cl_rs, out_sem,
):
    rows, width = tok.shape
    head = width // N
    part = width // NC
    hidden = win.shape[1]
    depth = xs.shape[2]
    group = depth * 4
    slots = N * depth
    tokens4 = N // NC
    dp = lax.axis_index("dp")
    ex = lax.axis_index("expert")
    z, co = dp // 2, dp % 2
    xm, ym = ex // 4, ex % 4

    def partner(r):
        return ((z + STEPS[r // 2] + RING) % RING) * 2 + (co + r % 2) % 2

    def load(src, dst, k):
        copy = pltpu.make_async_copy(src, dst, load_sem.at[k])
        copy.start()
        return copy

    got_tok = load(tok_h, tok, 0)
    got_win = load(win_h, win, 1)
    got_wout = load(wout_h, wout, 2)
    got_cot = load(cot_h, cot, 3)

    barrier = pltpu.get_barrier_semaphore()
    for r in range(1, N):
        pl.semaphore_signal(barrier, inc=1, device_id=(partner(r), ex), device_id_type=MESH)
    for k in range(1, N):
        pl.semaphore_signal(barrier, inc=1, device_id=(dp, (ex + k) % N), device_id_type=MESH)
    got_tok.wait()
    tok_t[...] = tok[...].T.reshape(N, head, rows)
    pl.semaphore_wait(barrier, 2 * (N - 1))

    mix_cp = {}
    for i in range(NC):
        for yy in range(4):
            k = i * 4 + yy
            to = ((xm - i + 4) % 4) * 4 + (ym + yy) % 4
            if k == 0:
                mix_t[ex] = tok_t[ex]
                continue
            mix_cp[k] = pltpu.make_async_remote_copy(
                src_ref=tok_t.at[to], dst_ref=mix_t.at[ex],
                send_sem=mix_ss.at[k], recv_sem=mix_rs.at[k],
                device_id=(dp, to), device_id_type=MESH,
            )
            mix_cp[k].start()

    ids0, ids1 = ids_ref[0:1, :], ids_ref[1:2, :]
    label = lax.broadcasted_iota(jnp.int32, (N, rows), 0)
    hot0 = (label == ids0).astype(F32)
    hot1 = (label == ids1).astype(F32)
    earlier = (
        lax.broadcasted_iota(jnp.int32, (rows, rows), 0)
        < lax.broadcasted_iota(jnp.int32, (rows, rows), 1)
    ).astype(F32)
    before = dot((hot0 + hot1).astype(BF16), earlier.astype(BF16))
    at0 = jnp.sum(before * hot0, axis=0, keepdims=True).astype(jnp.int32)
    at1 = jnp.sum(before * hot1, axis=0, keepdims=True).astype(jnp.int32)
    slot = lax.broadcasted_iota(jnp.int32, (depth, rows), 0)
    for g in range(NG):
        blocks = []
        for r in range(4 * g, 4 * g + 4):
            e = partner(r)
            goal0 = jnp.where(ids0 == e, at0, -1)
            goal1 = jnp.where(ids1 == e, at1, -1)
            blocks.append(jnp.logical_or(slot == goal0, slot == goal1).astype(F32))
        placed = jnp.concatenate(blocks, axis=0)
        place_m[g * group : (g + 1) * group, :] = placed.astype(BF16)
        place_t[g] = placed.T.astype(BF16)
    for c in range(NC):
        rt4[c] = rt_ref[:, c * part : (c + 1) * part]

    a_cp = {}
    for i in range(NC):
        c = (xm + i) % 4
        for yy in range(4):
            if i * 4 + yy:
                mix_cp[i * 4 + yy].wait_recv()
        mixed[c] = mix_t[pl.ds(c * tokens4, tokens4)].reshape(part, rows).T
        sent = dot(place_m[...], mixed[c]).astype(BF16).reshape(N, depth, part)
        xs[:, c] = sent
        xr[0, c] = sent[0]
        for r in range(1, N):
            a_cp[r, i] = pltpu.make_async_remote_copy(
                src_ref=xs.at[r, c], dst_ref=xr.at[inverse(r), c],
                send_sem=a_ss.at[r, i], recv_sem=a_rs.at[inverse(r), i],
                device_id=(partner(r), ex), device_id_type=MESH,
            )
            a_cp[r, i].start()

    got_win.wait()
    got_wout.wait()
    mine = lax.broadcasted_iota(jnp.int32, (group, N), 1) == dp
    for i in range(NC - 1):
        c = (xm + i) % 4
        for r in range(1, N):
            a_cp[inverse(r), i].wait_recv()
        for g in range(NG):
            at = slice(g * group, (g + 1) * group)
            block = xr[4 * g : 4 * g + 4, c].reshape(group, part)
            more = dot(block, win[pl.ds(pl.multiple_of(c * part, part), part), :])
            more_logit = dot_nt(block, rt4[c])
            if i == 0:
                pre[at, :] = more
                logit[at, :] = more_logit
            else:
                pre[at, :] += more
                logit[at, :] += more_logit
    b_cp = {}
    c = (xm + NC - 1) % 4
    for g in range(NG):
        at = slice(g * group, (g + 1) * group)
        for r in range(4 * g, 4 * g + 4):
            if r:
                a_cp[inverse(r), NC - 1].wait_recv()
        block = xr[4 * g : 4 * g + 4, c].reshape(group, part)
        value = pre[at, :] + dot(block, win[pl.ds(pl.multiple_of(c * part, part), part), :])
        score = logit[at, :] + dot_nt(block, rt4[c])
        share = jax.nn.sigmoid(jnp.sum(jnp.where(mine, score, 0.0), axis=1, keepdims=True))
        gate[at, :] = share
        activated, slope = gelu_and_slope(value)
        pre[at, :] = slope
        act[at, :] = activated.astype(BF16)
        for q in range(NC):
            out = dot(act[at, :], wout[:, q * part : (q + 1) * part])
            result = (share * out).astype(BF16).reshape(4, depth, part)
            ys[4 * g : 4 * g + 4, q] = result
            if g == 0:
                yr[0, q] = result[0]
        for r in range(4 * g, 4 * g + 4):
            if r:
                b_cp[r] = pltpu.make_async_remote_copy(
                    src_ref=ys.at[r], dst_ref=yr.at[inverse(r)],
                    send_sem=b_ss.at[r], recv_sem=b_rs.at[inverse(r)],
                    device_id=(partner(r), ex), device_id_type=MESH,
                )
                b_cp[r].start()

    for q in range(NC):
        acc[q] = mixed[q].astype(F32)
    for g in range(NG):
        for r in range(4 * g, 4 * g + 4):
            if r:
                b_cp[inverse(r)].wait_recv()
        for q in range(NC):
            acc[q] += dot(place_t[g], yr[4 * g : 4 * g + 4, q].reshape(group, part))

    got_cot.wait()
    ggp[...] = jnp.zeros_like(ggp)

    def norm_rows(j, carry):
        at = pl.ds(pl.multiple_of(j * TILE, TILE), TILE)
        cols = [slice(q * part, (q + 1) * part) for q in range(NC)]
        resid = [acc[q, at, :] for q in range(NC)]
        mean = sum(jnp.sum(v, axis=1, keepdims=True) for v in resid) / width
        resid = [v - mean for v in resid]
        var = sum(jnp.sum(v * v, axis=1, keepdims=True) for v in resid) / width
        inv_std = lax.rsqrt(var + norm_eps)
        normed = [v * inv_std for v in resid]
        grads, m1, m2 = [], 0.0, 0.0
        for q in range(NC):
            gain = gain_ref[0:1, cols[q]]
            norm_o[at, cols[q]] = (normed[q] * gain).astype(BF16)
            cot_f = cot[at, cols[q]].astype(F32)
            ggp[0:1, cols[q]] += jnp.sum(cot_f * normed[q], axis=0, keepdims=True)
            grad = cot_f * gain
            grads.append(grad)
            m1 += jnp.sum(grad, axis=1, keepdims=True)
            m2 += jnp.sum(grad * normed[q], axis=1, keepdims=True)
        m1, m2 = m1 / width, m2 / width
        for q in range(NC):
            grad = inv_std * (grads[q] - m1 - normed[q] * m2)
            acc[q, at, :] = grad
            grd[q, at, :] = grad.astype(BF16)
        return carry

    lax.fori_loop(0, rows // TILE, norm_rows, 0)

    for q in range(NC):
        sent = dot(place_m[...], grd[q]).astype(BF16).reshape(N, depth, part)
        gs[:, q] = sent
        gr[0, q] = sent[0]
    c_cp = {}
    for r in range(1, N):
        c_cp[r] = pltpu.make_async_remote_copy(
            src_ref=gs.at[r], dst_ref=gr.at[inverse(r)],
            send_sem=c_ss.at[r], recv_sem=c_rs.at[inverse(r)],
            device_id=(partner(r), ex), device_id_type=MESH,
        )
        c_cp[r].start()

    def spread(vector, source, target, gathered, send_sems, recv_sems):
        source[...] = jnp.zeros_like(source)
        for j in range(width // 128):
            source[j : j + 1, :] = vector[0:1, j * 128 : (j + 1) * 128]
        target[...] = source[...].astype(BF16)
        gathered[dp] = target[...]
        copies = {}
        for r in range(1, N):
            copies[r] = pltpu.make_async_remote_copy(
                src_ref=target, dst_ref=gathered.at[dp],
                send_sem=send_sems.at[r], recv_sem=recv_sems.at[inverse(r)],
                device_id=(partner(r), ex), device_id_type=MESH,
            )
            copies[r].start()
        return copies

    gn_cp = spread(ggp, small, gain_s, gain_r, gn_ss, gn_rs)
    put_norm = pltpu.make_async_copy(norm_o, no_h, out_sem.at[0])
    put_norm.start()

    rcol[...] = jnp.zeros_like(rcol)
    mine_row = lax.broadcasted_iota(jnp.int32, (N, part), 0) == dp
    d_cp = {}

    def send_back(r, i):
        c = (xm + 1 + i) % 4
        d_cp[r, i] = pltpu.make_async_remote_copy(
            src_ref=ds.at[r, c], dst_ref=dr.at[inverse(r), c],
            send_sem=d_ss.at[r, i], recv_sem=d_rs.at[inverse(r), i],
            device_id=(partner(r), ex), device_id_type=MESH,
        )
        d_cp[r, i].start()

    for g in range(NG):
        at = slice(g * group, (g + 1) * group)
        for r in range(4 * g, 4 * g + 4):
            if r:
                c_cp[inverse(r)].wait_recv()
        share = gate[at, :]
        grad_act, grad_gate = 0.0, 0.0
        for q in range(NC):
            grad = gr[4 * g : 4 * g + 4, q].reshape(group, part).astype(F32)
            result = ys[4 * g : 4 * g + 4, q].reshape(group, part).astype(F32)
            grad_gate += jnp.sum(grad * result, axis=1, keepdims=True)
            grad_out = (share * grad).astype(BF16)
            dos[q, at, :] = grad_out
            grad_act += dot_nt(grad_out, wout[:, q * part : (q + 1) * part])
        grad_logit = grad_gate * (1.0 - share)
        gp[at, :] = (grad_act * pre[at, :]).astype(BF16)
        for q in range(NC):
            weights = jnp.sum(jnp.where(mine_row, rt4[q].astype(F32), 0.0), axis=0, keepdims=True)
            back = dot_nt(gp[at, :], win[q * part : (q + 1) * part, :]) + grad_logit * weights
            back = back.astype(BF16).reshape(4, depth, part)
            ds[4 * g : 4 * g + 4, q] = back
            if g == 0:
                dr[0, q] = back[0]
            block = xr[4 * g : 4 * g + 4, q].reshape(group, part).astype(F32)
            rcol[0:1, q * part : (q + 1) * part] += jnp.sum(
                grad_logit * block, axis=0, keepdims=True
            )
        for i in range(2):
            for r in range(4 * g, 4 * g + 4):
                if r:
                    send_back(r, i)
    for i in range(2, NC):
        for r in range(1, N):
            send_back(r, i)
    cl_cp = spread(rcol, small, col_s, col_r, cl_ss, cl_rs)

    for q in range(NC):
        cols = slice(q * part, (q + 1) * part)
        gwi[cols, :] = dot_tn(xr[:, q].reshape(slots, part), gp[...]).astype(BF16)
        gwo[:, cols] = dot_tn(act[...], dos[q]).astype(BF16)
    put_gwi = pltpu.make_async_copy(gwi, gwi_h, out_sem.at[1])
    put_gwi.start()
    put_gwo = pltpu.make_async_copy(gwo, gwo_h, out_sem.at[2])
    put_gwo.start()

    e_cp = {}
    for i in range(NC):
        c = (xm + 1 + i) % 4
        for r in range(1, N):
            d_cp[inverse(r), i].wait_recv()
        total = acc[c]
        for g in range(NG):
            total += dot(place_t[g], dr[4 * g : 4 * g + 4, c].reshape(group, part))
        gm_t[pl.ds(c * tokens4, tokens4)] = total.astype(BF16).T.reshape(tokens4, head, rows)
        for yy in range(4):
            to = c * tokens4 + (ym + yy) % 4
            if i == NC - 1 and yy == 0:
                gt_t[ex] = gm_t[ex]
                continue
            k = i * 4 + yy
            e_cp[k] = pltpu.make_async_remote_copy(
                src_ref=gm_t.at[to], dst_ref=gt_t.at[ex],
                send_sem=e_ss.at[k], recv_sem=e_rs.at[k],
                device_id=(dp, to), device_id_type=MESH,
            )
            e_cp[k].start()

    for r in range(1, N):
        gn_cp[inverse(r)].wait_recv()
        cl_cp[inverse(r)].wait_recv()
    total = gain_r[0].astype(F32)
    for e in range(1, N):
        total += gain_r[e].astype(F32)
    small[...] = total
    for j in range(width // 128):
        gg_ref[0:1, j * 128 : (j + 1) * 128] = small[j : j + 1, :]
    for e in range(N):
        small[...] = col_r[e].astype(F32)
        for j in range(width // 128):
            gr_ref[e : e + 1, j * 128 : (j + 1) * 128] = small[j : j + 1, :]

    for k in e_cp:
        e_cp[k].wait_recv()
    gt_o[...] = gt_t[...].reshape(width, rows).T
    put_gt = pltpu.make_async_copy(gt_o, gt_h, out_sem.at[3])
    put_gt.start()
    for copies in (mix_cp, a_cp, b_cp, c_cp, d_cp, e_cp, gn_cp, cl_cp):
        for k in copies:
            copies[k].wait_send()
    put_norm.wait()
    put_gwi.wait()
    put_gwo.wait()
    put_gt.wait()


def body(tokens, route_ids, router, norm_gain, w_in, w_out, cotangent):
    rows, width = tokens.shape[0], tokens.shape[2]
    hidden = w_in.shape[3]
    depth = 3 * rows // N
    slots = N * depth
    part = width // NC
    head = width // N
    group = 4 * depth
    shape = jax.ShapeDtypeStruct
    vmem = pl.BlockSpec(memory_space=pltpu.VMEM)
    hbm = pl.BlockSpec(memory_space=pl.ANY)
    dma = pltpu.SemaphoreType.DMA
    blocks = pltpu.VMEM((N, NC, depth, part), BF16)
    flipped = pltpu.VMEM((N, head, rows), BF16)
    row_block = pltpu.VMEM((rows, width), BF16)
    out = pl.pallas_call(
        kernel,
        out_shape=(
            shape((rows, width), BF16),
            shape((rows, width), BF16),
            shape((N, width), F32),
            shape((1, width), F32),
            shape((width, hidden), BF16),
            shape((hidden, width), BF16),
        ),
        in_specs=[hbm, vmem, vmem, vmem, hbm, hbm, hbm],
        out_specs=[hbm, hbm, vmem, vmem, hbm, hbm],
        scratch_shapes=[
            row_block,
            flipped,
            flipped,
            pltpu.VMEM((NC, rows, part), BF16),
            row_block,
            pltpu.VMEM((width, hidden), BF16),
            pltpu.VMEM((hidden, width), BF16),
            pltpu.VMEM((NC, N, part), BF16),
            pltpu.VMEM((slots, rows), BF16),
            pltpu.VMEM((NG, rows, group), BF16),
            blocks,
            blocks,
            pltpu.VMEM((slots, hidden), F32),
            pltpu.VMEM((slots, N), F32),
            pltpu.VMEM((slots, 1), F32),
            pltpu.VMEM((slots, hidden), BF16),
            blocks,
            blocks,
            pltpu.VMEM((NC, rows, part), F32),
            pltpu.VMEM((NC, rows, part), BF16),
            blocks,
            blocks,
            pltpu.VMEM((slots, hidden), BF16),
            pltpu.VMEM((NC, slots, part), BF16),
            blocks,
            blocks,
            row_block,
            pltpu.VMEM((width, hidden), BF16),
            pltpu.VMEM((hidden, width), BF16),
            flipped,
            flipped,
            row_block,
            pltpu.VMEM((8, width), F32),
            pltpu.VMEM((8, width), F32),
            pltpu.VMEM((16, 128), F32),
            pltpu.VMEM((16, 128), BF16),
            pltpu.VMEM((N, 16, 128), BF16),
            pltpu.VMEM((16, 128), BF16),
            pltpu.VMEM((N, 16, 128), BF16),
            dma((4,)),
            dma((N,)), dma((N,)),
            dma((N, NC)), dma((N, NC)),
            dma((N,)), dma((N,)),
            dma((N,)), dma((N,)),
            dma((N, NC)), dma((N, NC)),
            dma((N,)), dma((N,)),
            dma((N,)), dma((N,)),
            dma((N,)), dma((N,)),
            dma((4,)),
        ],
        name="rank_mixer",
        compiler_params=pltpu.CompilerParams(
            collective_id=0, has_side_effects=True, vmem_limit_bytes=60 << 20
        ),
    )(
        tokens.reshape(rows, width),
        route_ids.reshape(rows, 2).T,
        router.reshape(width, N).T,
        norm_gain.reshape(1, width),
        w_in.reshape(width, hidden),
        w_out.reshape(hidden, width),
        cotangent.reshape(rows, width),
    )
    normed_out, grad_tokens, grad_router, grad_gain, grad_w_in, grad_w_out = out
    return (
        normed_out.reshape(rows, 1, width),
        grad_tokens.reshape(rows, 1, width),
        grad_router.T.reshape(1, width, N),
        grad_gain,
        grad_w_in.reshape(1, 1, width, hidden),
        grad_w_out.reshape(1, 1, hidden, width),
    )


def solution(mesh):
    return jax.shard_map(
        body,
        mesh=mesh,
        in_specs=(
            P("dp", "expert", None),
            P("expert", "dp", None),
            P("expert", None, None),
            P("expert", None),
            P("expert", "dp", None, None),
            P("expert", "dp", None, None),
            P("dp", "expert", None),
        ),
        out_specs=(
            P("dp", "expert", None),
            P("dp", "expert", None),
            P("expert", None, None),
            P("expert", None),
            P("expert", "dp", None, None),
            P("expert", "dp", None, None),
        ),
        check_vma=False,
    )
```

time: 350 us -> 257 us (0.73)
  Pallas kernels: 0 us -> 246 us
  blocking collectives: 211 us -> 0 us
  waiting for transfers between devices: 66.9 us -> 0 us
  matrix products: 35.2 us -> 0 us
  starting transfers between devices: 20.2 us -> 0 us
  other arithmetic: 5.39 us -> 0 us
    pallas_call x0 -> x1, Pallas kernels: none -> 246 us  [body(): pl.pallas_call(kernel, out_shape=(shape((rows, width), BF16), shape((rows...]
    all_to_all x2 -> x0, blocking collectives: 130 us -> none  [the longest x1 67.6 us: body(): lax.all_to_all(outgoing, 'dp', split_axis=0, concat_axis=0, tiled=True)]
    all_gather x2 -> x0, blocking collectives: 81.6 us -> none  [gathered_total(): return lax.all_gather(value, axis).astype(jnp.float32).sum(0)]
    all_to_all x4 -> x0, waiting for transfers between devices: 66.9 us -> none  [the longest x1 51.9 us: send_back(): return lax.all_to_all(result, 'dp', split_axis=0, concat_axis=0, tiled=True)]
    dot_general x15 -> x0, matrix products: 35.2 us -> none  [the longest x6 19.9 us: pick_rows(): lax.dot_general(hot, rows, (((0,), (0,)), ((), ())), preferred_element_ty...]
    all_to_all x4 -> x0, starting transfers between devices: 20.2 us -> none  [the longest x1 7.58 us: body(): lax.all_to_all(own_rows, 'expert', split_axis=1, concat_axis=1, tiled=True)]
    reduce_sum x9 -> x0, other arithmetic: 4 us -> none  [the longest x1 1.68 us: body(): first_grad = jnp.sum(grad_resid * first_out, axis=1)]
    unnamed x37 -> x14, local copies, waits for them, and re-layouts: 6.11 us -> 9.44 us
  transfers between devices with their start and end apart: 4 -> 0, of which waited for: 3 -> 0; matrix products, arithmetic and copies ran while one was open for 5% -> 0% of each run, Pallas kernels for 0% -> 0%
where the time goes in v1:
time: 257 us; the launch traced here: 256 us
  Pallas kernels  246 us (96%)
  local copies, waits for them, and re-layouts  9.44 us (4%)
    pallas_call x1, Pallas kernels, body(): pl.pallas_call(kernel, out_shape=(shape((rows, width), BF16), shape((rows...  246 us
    unnamed x14, local copies, waits for them, and re-layouts  9.44 us

profile of v1, /device:TPU:1, one launch (start us, length us, event | category | flops | bytes accessed | tf_op | source)
XLA Modules:
  0.0 256.0 jit_solution(16948107905277719294)
XLA Ops:
  0.6 245.8 %rank_mixer.1 = (bf16[256,1536]{1,0:T(8,128)(2,1)}, bf16[256,1536]{1,0:T(8,128)(2,1)}, f32[16,1536]{1,0:T(8,128)}, f32[1,1536]{1,0:T(1,128)}, bf16[1536,768]{1,0:T(8,128)(2,1)}, /*index=5*/bf16[768,1536]{1,0:T(8,128)(2,1)}) custom-call(bf16[256,1536]{1,0:T(8,128)(2,1)} %bitcast.21, s32[2,256]{1,0:T(2,128)} %bitcast.27, bf16[16,1536]{1,0:T(8,128)(2,1)} %bitcast.26, ...), custom_call_target="tpu_custom_call" | custom-call | tf_op jit(solution)/shard_map/rank_mixer/pallas_call | solution.py:400
  246.5 0.0 copy-start.2
  246.5 0.0 copy-start.3
  246.5 0.0 copy-start.1
  246.5 2.2 copy.19
  248.7 2.1 copy.20
  250.8 0.0 copy-done.2
  250.8 0.6 copy.21
  251.4 0.0 copy-done.3
  251.4 0.6 copy.22
  252.0 0.0 copy-done.1
  252.0 0.0 copy-start
  252.0 1.4 copy.23
  253.4 1.1 copy-done
  254.5 1.4 copy.24
Async XLA Ops:
  246.5 4.3 %copy-start.2 = (f32[16,1536]{1,0:T(8,128)S(1)}, f32[16,1536]{1,0:T(8,128)}, u32[]{:S(2)}) copy-start(f32[16,1536]{1,0:T(8,128)} %get-tuple-element.14) | copy-start | bytes 294916
  246.5 4.9 %copy-start.3 = (f32[1,1536]{1,0:T(1,128)S(1)}, f32[1,1536]{1,0:T(1,128)}, u32[]{:S(2)}) copy-start(f32[1,1536]{1,0:T(1,128)} %get-tuple-element.27) | copy-start | bytes 18436
  246.5 5.5 %copy-start.1 = (bf16[1536,768]{1,0:T(8,128)(2,1)S(1)}, bf16[1536,768]{1,0:T(8,128)(2,1)}, u32[]{:S(2)}) copy-start(bf16[1536,768]{1,0:T(8,128)(2,1)} %get-tuple-element.16) | copy-start | bytes 7077892
  252.0 2.5 copy-start

commit v2 on v1

--- a/solution.py
+++ b/solution.py
@@ -21,7 +21,14 @@
 RING = 8
 STEPS = (0, 1, -1, 2, -2, 3, -3, 4)
 BACK = (0, 2, 1, 4, 3, 6, 5, 7)
+HOPS = (0, 0, 0, 0, 0, 0, -1, -1, 1, 1, -2, -2, 2, 2, 3, -3)
+FROM_LOW = (4, 5, 8, 9, 12, 13, 14)
+FROM_HIGH = (2, 3, 6, 7, 10, 11, 15)
+OWN = (0, 1)
+HERE = (0, 2, 4)
+AWAY = tuple(r for r in range(N) if r not in HERE)
 TILE = 32
+RUNS = 4
 
 
 def inverse(r):
@@ -53,11 +60,15 @@
 def kernel(
     tok_h, ids_ref, rt_ref, gain_ref, win_h, wout_h, cot_h,
     no_h, gt_h, gr_ref, gg_ref, gwi_h, gwo_h,
-    tok, tok_t, mix_t, mixed, cot, win, wout, rt4, place_m, place_t,
-    xs, xr, pre, logit, gate, act, ys, yr, acc, grd, gs, gr, gp, dos, ds, dr,
+    tok, tok_t, mix_t, mixed, cot, win, wout, rt4,
+    ids_o, ids_l, ids_h, pl_m, ph_m, po_m, pl_t, ph_t, po_t,
+    raw_l, raw_h, xs, xr, pre, logit, gate, act, ys, yr,
+    part_l, part_h, sum_h, sum_l, acc, grd, raw2_l, raw2_h, gs, gr, gp, dos, ds, dr,
+    part2_l, part2_h, sum2_h, sum2_l,
     norm_o, gwi, gwo, gm_t, gt_t, gt_o, ggp, rcol, small,
     gain_s, gain_r, col_s, col_r,
-    load_sem, mix_ss, mix_rs, a_ss, a_rs, b_ss, b_rs, c_ss, c_rs, d_ss, d_rs,
+    load_sem, ids_ss, ids_rs, mix_ss, mix_rs, raw_ss, raw_rs, a_ss, a_rs, b_ss, b_rs,
+    sum_ss, sum_rs, raw2_ss, raw2_rs, c_ss, c_rs, d_ss, d_rs, sum2_ss, sum2_rs,
     e_ss, e_rs, gn_ss, gn_rs, cl_ss, cl_rs, out_sem,
 ):
     rows, width = tok.shape
@@ -76,6 +87,23 @@
     def partner(r):
         return ((z + STEPS[r // 2] + RING) % RING) * 2 + (co + r % 2) % 2
 
+    def target(r):
+        return ((z + HOPS[r] + RING) % RING) * 2 + (co + r % 2) % 2
+
+    def origin(r):
+        return ((z - HOPS[r] + RING) % RING) * 2 + (co + r % 2) % 2
+
+    high = ((z + 1) % RING) * 2 + co
+    low = ((z + RING - 1) % RING) * 2 + co
+
+    def send(src, dst, send_sem, recv_sem, to):
+        copy = pltpu.make_async_remote_copy(
+            src_ref=src, dst_ref=dst, send_sem=send_sem, recv_sem=recv_sem,
+            device_id=(to, ex), device_id_type=MESH,
+        )
+        copy.start()
+        return copy
+
     def load(src, dst, k):
         copy = pltpu.make_async_copy(src, dst, load_sem.at[k])
         copy.start()
@@ -93,7 +121,13 @@
         pl.semaphore_signal(barrier, inc=1, device_id=(dp, (ex + k) % N), device_id_type=MESH)
     got_tok.wait()
     tok_t[...] = tok[...].T.reshape(N, head, rows)
+    ids_o[...] = jnp.zeros_like(ids_o)
+    ids_o[0:2, :] = ids_ref[...]
     pl.semaphore_wait(barrier, 2 * (N - 1))
+    ids_cp = {
+        0: send(ids_o, ids_l, ids_ss.at[0], ids_rs.at[0], high),
+        1: send(ids_o, ids_h, ids_ss.at[1], ids_rs.at[1], low),
+    }
 
     mix_cp = {}
     for i in range(NC):
@@ -110,56 +144,87 @@
             )
             mix_cp[k].start()
 
-    ids0, ids1 = ids_ref[0:1, :], ids_ref[1:2, :]
     label = lax.broadcasted_iota(jnp.int32, (N, rows), 0)
-    hot0 = (label == ids0).astype(F32)
-    hot1 = (label == ids1).astype(F32)
     earlier = (
         lax.broadcasted_iota(jnp.int32, (rows, rows), 0)
         < lax.broadcasted_iota(jnp.int32, (rows, rows), 1)
     ).astype(F32)
-    before = dot((hot0 + hot1).astype(BF16), earlier.astype(BF16))
-    at0 = jnp.sum(before * hot0, axis=0, keepdims=True).astype(jnp.int32)
-    at1 = jnp.sum(before * hot1, axis=0, keepdims=True).astype(jnp.int32)
+    earlier = earlier.astype(BF16)
     slot = lax.broadcasted_iota(jnp.int32, (depth, rows), 0)
-    for g in range(NG):
+
+    def place(ids, members, matrix, flipped):
+        ids0, ids1 = ids[0:1, :], ids[1:2, :]
+        hot0 = (label == ids0).astype(F32)
+        hot1 = (label == ids1).astype(F32)
+        before = dot((hot0 + hot1).astype(BF16), earlier)
+        at0 = jnp.sum(before * hot0, axis=0, keepdims=True).astype(jnp.int32)
+        at1 = jnp.sum(before * hot1, axis=0, keepdims=True).astype(jnp.int32)
         blocks = []
-        for r in range(4 * g, 4 * g + 4):
-            e = partner(r)
+        for r in members:
+            e = target(r)
             goal0 = jnp.where(ids0 == e, at0, -1)
             goal1 = jnp.where(ids1 == e, at1, -1)
             blocks.append(jnp.logical_or(slot == goal0, slot == goal1).astype(F32))
         placed = jnp.concatenate(blocks, axis=0)
-        place_m[g * group : (g + 1) * group, :] = placed.astype(BF16)
-        place_t[g] = placed.T.astype(BF16)
+        matrix[...] = placed.astype(BF16)
+        flipped[...] = placed.T.astype(BF16)
+
+    def stack(blocks, members, q):
+        return jnp.concatenate([blocks[r, q] for r in members], axis=0)
+
+    def expand(matrix, values, members, q, out, arrived):
+        sent = dot(matrix[...], values).astype(BF16)
+        for n, r in enumerate(members):
+            into = arrived if r in HERE else out
+            into[r, q] = sent[n * depth : (n + 1) * depth]
+
+    place(ids_o, OWN, po_m, po_t)
     for c in range(NC):
         rt4[c] = rt_ref[:, c * part : (c + 1) * part]
-
-    a_cp = {}
-    for i in range(NC):
+    ids_cp[0].wait_recv()
+    ids_cp[1].wait_recv()
+    place(ids_l, FROM_LOW, pl_m, pl_t)
+    place(ids_h, FROM_HIGH, ph_m, ph_t)
+
+    raw_cp, a_cp = {}, {}
+
+    def send_mixed(r, i):
+        c = (xm + i) % 4
+        a_cp[r, i] = send(xs.at[r, c], xr.at[r, c], a_ss.at[r, i], a_rs.at[r, i], target(r))
+
+    def mix_chunk(i):
         c = (xm + i) % 4
         for yy in range(4):
             if i * 4 + yy:
                 mix_cp[i * 4 + yy].wait_recv()
         mixed[c] = mix_t[pl.ds(c * tokens4, tokens4)].reshape(part, rows).T
-        sent = dot(place_m[...], mixed[c]).astype(BF16).reshape(N, depth, part)
-        xs[:, c] = sent
-        xr[0, c] = sent[0]
-        for r in range(1, N):
-            a_cp[r, i] = pltpu.make_async_remote_copy(
-                src_ref=xs.at[r, c], dst_ref=xr.at[inverse(r), c],
-                send_sem=a_ss.at[r, i], recv_sem=a_rs.at[inverse(r), i],
-                device_id=(partner(r), ex), device_id_type=MESH,
-            )
-            a_cp[r, i].start()
+        raw_cp[0, i] = send(mixed.at[c], raw_l.at[c], raw_ss.at[0, i], raw_rs.at[0, i], high)
+        raw_cp[1, i] = send(mixed.at[c], raw_h.at[c], raw_ss.at[1, i], raw_rs.at[1, i], low)
+        expand(po_m, mixed[c], OWN, c, xs, xr)
+        send_mixed(1, i)
+
+    def pass_on(i):
+        c = (xm + i) % 4
+        raw_cp[0, i].wait_recv()
+        expand(pl_m, raw_l[c], FROM_LOW, c, xs, xr)
+        raw_cp[1, i].wait_recv()
+        expand(ph_m, raw_h[c], FROM_HIGH, c, xs, xr)
+        for r in AWAY[1:]:
+            send_mixed(r, i)
+
+    for i in range(NC):
+        mix_chunk(i)
+        if i:
+            pass_on(i - 1)
+    pass_on(NC - 1)
 
     got_win.wait()
     got_wout.wait()
     mine = lax.broadcasted_iota(jnp.int32, (group, N), 1) == dp
     for i in range(NC - 1):
         c = (xm + i) % 4
-        for r in range(1, N):
-            a_cp[inverse(r), i].wait_recv()
+        for r in AWAY:
+            a_cp[r, i].wait_recv()
         for g in range(NG):
             at = slice(g * group, (g + 1) * group)
             block = xr[4 * g : 4 * g + 4, c].reshape(group, part)
@@ -176,8 +241,8 @@
     for g in range(NG):
         at = slice(g * group, (g + 1) * group)
         for r in range(4 * g, 4 * g + 4):
-            if r:
-                a_cp[inverse(r), NC - 1].wait_recv()
+            if r in AWAY:
+                a_cp[r, NC - 1].wait_recv()
         block = xr[4 * g : 4 * g + 4, c].reshape(group, part)
         value = pre[at, :] + dot(block, win[pl.ds(pl.multiple_of(c * part, part), part), :])
         score = logit[at, :] + dot_nt(block, rt4[c])
@@ -190,33 +255,33 @@
             out = dot(act[at, :], wout[:, q * part : (q + 1) * part])
             result = (share * out).astype(BF16).reshape(4, depth, part)
             ys[4 * g : 4 * g + 4, q] = result
-            if g == 0:
-                yr[0, q] = result[0]
+            for r in range(4 * g, 4 * g + 4):
+                if r in HERE:
+                    yr[r, q] = result[r - 4 * g]
         for r in range(4 * g, 4 * g + 4):
-            if r:
-                b_cp[r] = pltpu.make_async_remote_copy(
-                    src_ref=ys.at[r], dst_ref=yr.at[inverse(r)],
-                    send_sem=b_ss.at[r], recv_sem=b_rs.at[inverse(r)],
-                    device_id=(partner(r), ex), device_id_type=MESH,
-                )
-                b_cp[r].start()
-
+            if r in AWAY:
+                b_cp[r] = send(ys.at[r], yr.at[r], b_ss.at[r], b_rs.at[r], origin(r))
+
+    sum_cp = {}
+    for r in AWAY:
+        b_cp[r].wait_recv()
     for q in range(NC):
-        acc[q] = mixed[q].astype(F32)
-    for g in range(NG):
-        for r in range(4 * g, 4 * g + 4):
-            if r:
-                b_cp[inverse(r)].wait_recv()
-        for q in range(NC):
-            acc[q] += dot(place_t[g], yr[4 * g : 4 * g + 4, q].reshape(group, part))
-
+        part_l[q] = dot(pl_t[...], stack(yr, FROM_LOW, q)).astype(BF16)
+        sum_cp[0, q] = send(part_l.at[q], sum_h.at[q], sum_ss.at[0, q], sum_rs.at[0, q], low)
+        part_h[q] = dot(ph_t[...], stack(yr, FROM_HIGH, q)).astype(BF16)
+        sum_cp[1, q] = send(part_h.at[q], sum_l.at[q], sum_ss.at[1, q], sum_rs.at[1, q], high)
+    for q in range(NC):
+        acc[q] = mixed[q].astype(F32) + dot(po_t[...], stack(yr, OWN, q))
     got_cot.wait()
     ggp[...] = jnp.zeros_like(ggp)
 
     def norm_rows(j, carry):
         at = pl.ds(pl.multiple_of(j * TILE, TILE), TILE)
         cols = [slice(q * part, (q + 1) * part) for q in range(NC)]
-        resid = [acc[q, at, :] for q in range(NC)]
+        resid = [
+            acc[q, at, :] + sum_h[q, at, :].astype(F32) + sum_l[q, at, :].astype(F32)
+            for q in range(NC)
+        ]
         mean = sum(jnp.sum(v, axis=1, keepdims=True) for v in resid) / width
         resid = [v - mean for v in resid]
         var = sum(jnp.sum(v * v, axis=1, keepdims=True) for v in resid) / width
@@ -239,20 +304,18 @@
             grd[q, at, :] = grad.astype(BF16)
         return carry
 
-    lax.fori_loop(0, rows // TILE, norm_rows, 0)
-
     for q in range(NC):
-        sent = dot(place_m[...], grd[q]).astype(BF16).reshape(N, depth, part)
-        gs[:, q] = sent
-        gr[0, q] = sent[0]
-    c_cp = {}
-    for r in range(1, N):
-        c_cp[r] = pltpu.make_async_remote_copy(
-            src_ref=gs.at[r], dst_ref=gr.at[inverse(r)],
-            send_sem=c_ss.at[r], recv_sem=c_rs.at[inverse(r)],
-            device_id=(partner(r), ex), device_id_type=MESH,
-        )
-        c_cp[r].start()
+        sum_cp[0, q].wait_recv()
+        sum_cp[1, q].wait_recv()
+
+    raw2_cp, c_cp = {}, {}
+    run = rows // RUNS
+    for i in range(RUNS):
+        lax.fori_loop(i * run // TILE, (i + 1) * run // TILE, norm_rows, 0)
+        src = grd.at[:, i * run : (i + 1) * run, :]
+        to_high, to_low = (d.at[:, i * run : (i + 1) * run, :] for d in (raw2_l, raw2_h))
+        raw2_cp[0, i] = send(src, to_high, raw2_ss.at[0, i], raw2_rs.at[0, i], high)
+        raw2_cp[1, i] = send(src, to_low, raw2_ss.at[1, i], raw2_rs.at[1, i], low)
 
     def spread(vector, source, target, gathered, send_sems, recv_sems):
         source[...] = jnp.zeros_like(source)
@@ -273,6 +336,16 @@
     gn_cp = spread(ggp, small, gain_s, gain_r, gn_ss, gn_rs)
     put_norm = pltpu.make_async_copy(norm_o, no_h, out_sem.at[0])
     put_norm.start()
+    for q in range(NC):
+        expand(po_m, grd[q], OWN, q, gs, gr)
+    for i in range(RUNS):
+        raw2_cp[0, i].wait_recv()
+        raw2_cp[1, i].wait_recv()
+    for q in range(NC):
+        expand(pl_m, raw2_l[q], FROM_LOW, q, gs, gr)
+        expand(ph_m, raw2_h[q], FROM_HIGH, q, gs, gr)
+    for r in AWAY:
+        c_cp[r] = send(gs.at[r], gr.at[r], c_ss.at[r], c_rs.at[r], target(r))
 
     rcol[...] = jnp.zeros_like(rcol)
     mine_row = lax.broadcasted_iota(jnp.int32, (N, part), 0) == dp
@@ -280,18 +353,13 @@
 
     def send_back(r, i):
         c = (xm + 1 + i) % 4
-        d_cp[r, i] = pltpu.make_async_remote_copy(
-            src_ref=ds.at[r, c], dst_ref=dr.at[inverse(r), c],
-            send_sem=d_ss.at[r, i], recv_sem=d_rs.at[inverse(r), i],
-            device_id=(partner(r), ex), device_id_type=MESH,
-        )
-        d_cp[r, i].start()
+        d_cp[r, i] = send(ds.at[r, c], dr.at[r, c], d_ss.at[r, i], d_rs.at[r, i], origin(r))
 
     for g in range(NG):
         at = slice(g * group, (g + 1) * group)
         for r in range(4 * g, 4 * g + 4):
-            if r:
-                c_cp[inverse(r)].wait_recv()
+            if r in AWAY:
+                c_cp[r].wait_recv()
         share = gate[at, :]
         grad_act, grad_gate = 0.0, 0.0
         for q in range(NC):
@@ -308,18 +376,19 @@
             back = dot_nt(gp[at, :], win[q * part : (q + 1) * part, :]) + grad_logit * weights
             back = back.astype(BF16).reshape(4, depth, part)
             ds[4 * g : 4 * g + 4, q] = back
-            if g == 0:
-                dr[0, q] = back[0]
+            for r in range(4 * g, 4 * g + 4):
+                if r in HERE:
+                    dr[r, q] = back[r - 4 * g]
             block = xr[4 * g : 4 * g + 4, q].reshape(group, part).astype(F32)
             rcol[0:1, q * part : (q + 1) * part] += jnp.sum(
                 grad_logit * block, axis=0, keepdims=True
             )
         for i in range(2):
             for r in range(4 * g, 4 * g + 4):
-                if r:
+                if r in AWAY:
                     send_back(r, i)
     for i in range(2, NC):
-        for r in range(1, N):
+        for r in AWAY:
             send_back(r, i)
     cl_cp = spread(rcol, small, col_s, col_r, cl_ss, cl_rs)
 
@@ -332,14 +401,23 @@
     put_gwo = pltpu.make_async_copy(gwo, gwo_h, out_sem.at[2])
     put_gwo.start()
 
-    e_cp = {}
-    for i in range(NC):
+    sum2_cp, e_cp = {}, {}
+
+    def sum_back(i):
         c = (xm + 1 + i) % 4
-        for r in range(1, N):
-            d_cp[inverse(r), i].wait_recv()
-        total = acc[c]
-        for g in range(NG):
-            total += dot(place_t[g], dr[4 * g : 4 * g + 4, c].reshape(group, part))
+        for r in AWAY:
+            d_cp[r, i].wait_recv()
+        part2_l[c] = dot(pl_t[...], stack(dr, FROM_LOW, c)).astype(BF16)
+        sum2_cp[0, i] = send(part2_l.at[c], sum2_h.at[c], sum2_ss.at[0, i], sum2_rs.at[0, i], low)
+        part2_h[c] = dot(ph_t[...], stack(dr, FROM_HIGH, c)).astype(BF16)
+        sum2_cp[1, i] = send(part2_h.at[c], sum2_l.at[c], sum2_ss.at[1, i], sum2_rs.at[1, i], high)
+        acc[c] += dot(po_t[...], stack(dr, OWN, c))
+
+    def finish_chunk(i):
+        c = (xm + 1 + i) % 4
+        sum2_cp[0, i].wait_recv()
+        sum2_cp[1, i].wait_recv()
+        total = acc[c] + sum2_h[c].astype(F32) + sum2_l[c].astype(F32)
         gm_t[pl.ds(c * tokens4, tokens4)] = total.astype(BF16).T.reshape(tokens4, head, rows)
         for yy in range(4):
             to = c * tokens4 + (ym + yy) % 4
@@ -354,6 +432,12 @@
             )
             e_cp[k].start()
 
+    for i in range(NC):
+        sum_back(i)
+        if i:
+            finish_chunk(i - 1)
+    finish_chunk(NC - 1)
+
     for r in range(1, N):
         gn_cp[inverse(r)].wait_recv()
         cl_cp[inverse(r)].wait_recv()
@@ -373,7 +457,9 @@
     gt_o[...] = gt_t[...].reshape(width, rows).T
     put_gt = pltpu.make_async_copy(gt_o, gt_h, out_sem.at[3])
     put_gt.start()
-    for copies in (mix_cp, a_cp, b_cp, c_cp, d_cp, e_cp, gn_cp, cl_cp):
+    for copies in (
+        ids_cp, mix_cp, raw_cp, a_cp, b_cp, sum_cp, raw2_cp, c_cp, d_cp, sum2_cp, e_cp, gn_cp, cl_cp,
+    ):
         for k in copies:
             copies[k].wait_send()
     put_norm.wait()
@@ -397,6 +483,8 @@
     blocks = pltpu.VMEM((N, NC, depth, part), BF16)
     flipped = pltpu.VMEM((N, head, rows), BF16)
     row_block = pltpu.VMEM((rows, width), BF16)
+    chunks = pltpu.VMEM((NC, rows, part), BF16)
+    ids = pltpu.VMEM((8, rows), jnp.int32)
     out = pl.pallas_call(
         kernel,
         out_shape=(
@@ -413,13 +501,19 @@
             row_block,
             flipped,
             flipped,
-            pltpu.VMEM((NC, rows, part), BF16),
+            chunks,
             row_block,
             pltpu.VMEM((width, hidden), BF16),
             pltpu.VMEM((hidden, width), BF16),
             pltpu.VMEM((NC, N, part), BF16),
-            pltpu.VMEM((slots, rows), BF16),
-            pltpu.VMEM((NG, rows, group), BF16),
+            ids, ids, ids,
+            pltpu.VMEM((7 * depth, rows), BF16),
+            pltpu.VMEM((7 * depth, rows), BF16),
+            pltpu.VMEM((2 * depth, rows), BF16),
+            pltpu.VMEM((rows, 7 * depth), BF16),
+            pltpu.VMEM((rows, 7 * depth), BF16),
+            pltpu.VMEM((rows, 2 * depth), BF16),
+            chunks, chunks,
             blocks,
             blocks,
             pltpu.VMEM((slots, hidden), F32),
@@ -428,14 +522,17 @@
             pltpu.VMEM((slots, hidden), BF16),
             blocks,
             blocks,
+            chunks, chunks, chunks, chunks,
             pltpu.VMEM((NC, rows, part), F32),
-            pltpu.VMEM((NC, rows, part), BF16),
+            chunks,
+            chunks, chunks,
             blocks,
             blocks,
             pltpu.VMEM((slots, hidden), BF16),
             pltpu.VMEM((NC, slots, part), BF16),
             blocks,
             blocks,
+            chunks, chunks, chunks, chunks,
             row_block,
             pltpu.VMEM((width, hidden), BF16),
             pltpu.VMEM((hidden, width), BF16),
@@ -450,11 +547,16 @@
             pltpu.VMEM((16, 128), BF16),
             pltpu.VMEM((N, 16, 128), BF16),
             dma((4,)),
+            dma((2,)), dma((2,)),
+            dma((N,)), dma((N,)),
+            dma((2, NC)), dma((2, NC)),
+            dma((N, NC)), dma((N, NC)),
+            dma((N,)), dma((N,)),
+            dma((2, NC)), dma((2, NC)),
+            dma((2, RUNS)), dma((2, RUNS)),
             dma((N,)), dma((N,)),
             dma((N, NC)), dma((N, NC)),
-            dma((N,)), dma((N,)),
-            dma((N,)), dma((N,)),
-            dma((N, NC)), dma((N, NC)),
+            dma((2, NC)), dma((2, NC)),
             dma((N,)), dma((N,)),
             dma((N,)), dma((N,)),
             dma((N,)), dma((N,)),

time: 257 us -> 242 us (0.942)
  Pallas kernels: 246 us -> 232 us
    pallas_call x1, Pallas kernels: 246 us -> 232 us  [body(): pl.pallas_call(kernel, out_shape=(shape((rows, width), BF16), shape((rows...]
where the time goes in v2:
time: 242 us
  Pallas kernels  232 us (96%)
  local copies, waits for them, and re-layouts  9.44 us (4%)
    pallas_call x1, Pallas kernels, body(): pl.pallas_call(kernel, out_shape=(shape((rows, width), BF16), shape((rows...  232 us
    unnamed x14, local copies, waits for them, and re-layouts  9.44 us

profile of v2, /device:TPU:1, one launch (start us, length us, event | category | flops | bytes accessed | tf_op | source)
XLA Modules:
  0.0 241.6 jit_solution(16935688904864346243)
XLA Ops:
  0.6 231.5 %rank_mixer.1 = (bf16[256,1536]{1,0:T(8,128)(2,1)}, bf16[256,1536]{1,0:T(8,128)(2,1)}, f32[16,1536]{1,0:T(8,128)}, f32[1,1536]{1,0:T(1,128)}, bf16[1536,768]{1,0:T(8,128)(2,1)}, /*index=5*/bf16[768,1536]{1,0:T(8,128)(2,1)}) custom-call(bf16[256,1536]{1,0:T(8,128)(2,1)} %bitcast.21, s32[2,256]{1,0:T(2,128)} %bitcast.27, bf16[16,1536]{1,0:T(8,128)(2,1)} %bitcast.26, ...), custom_call_target="tpu_custom_call" | custom-call | tf_op jit(solution)/shard_map/rank_mixer/pallas_call | solution.py:488
  232.2 0.0 copy-start.2
  232.2 0.0 copy-start.3
  232.2 0.0 copy-start.1
  232.2 2.2 copy.19
  234.4 2.1 copy.20
  236.5 0.0 copy-done.2
  236.5 0.6 copy.21
  237.1 0.0 copy-done.3
  237.1 0.6 copy.22
  237.7 0.0 copy-done.1
  237.7 0.0 copy-start
  237.7 1.4 copy.23
  239.1 1.1 copy-done
  240.2 1.4 copy.24
Async XLA Ops:
  232.2 4.3 %copy-start.2 = (f32[16,1536]{1,0:T(8,128)S(1)}, f32[16,1536]{1,0:T(8,128)}, u32[]{:S(2)}) copy-start(f32[16,1536]{1,0:T(8,128)} %get-tuple-element.14) | copy-start | bytes 294916
  232.2 4.9 %copy-start.3 = (f32[1,1536]{1,0:T(1,128)S(1)}, f32[1,1536]{1,0:T(1,128)}, u32[]{:S(2)}) copy-start(f32[1,1536]{1,0:T(1,128)} %get-tuple-element.27) | copy-start | bytes 18436
  232.2 5.5 %copy-start.1 = (bf16[1536,768]{1,0:T(8,128)(2,1)S(1)}, bf16[1536,768]{1,0:T(8,128)(2,1)}, u32[]{:S(2)}) copy-start(bf16[1536,768]{1,0:T(8,128)(2,1)} %get-tuple-element.16) | copy-start | bytes 7077892
  237.7 2.5 %copy-start = (bf16[768,1536]{1,0:T(8,128)(2,1)S(1)}, bf16[768,1536]{1,0:T(8,128)(2,1)}, u32[]{:S(2)}) copy-start(bf16[768,1536]{1,0:T(8,128)(2,1)} %get-tuple-element.17) | copy-start | bytes 7077892

commit v3 on v2

--- a/solution.py
+++ b/solution.py
@@ -58,14 +58,13 @@
 
 
 def kernel(
-    tok_h, ids_ref, rt_ref, gain_ref, win_h, wout_h, cot_h,
+    tok_h, ids_h, rt_h, gain_h, win_h, wout_h, cot_h,
     no_h, gt_h, gr_ref, gg_ref, gwi_h, gwo_h,
-    tok, tok_t, mix_t, mixed, cot, win, wout, rt4,
-    ids_o, ids_l, ids_h, pl_m, ph_m, po_m, pl_t, ph_t, po_t,
+    tok, ids_ref, rt_ref, gain_ref, tok_t, mix_t, mixed, cot, win, wout, rt4,
+    ids_own, ids_low, ids_high, pl_m, ph_m, po_m, pl_t, ph_t, po_t,
     raw_l, raw_h, xs, xr, pre, logit, gate, act, ys, yr,
-    part_l, part_h, sum_h, sum_l, acc, grd, raw2_l, raw2_h, gs, gr, gp, dos, ds, dr,
-    part2_l, part2_h, sum2_h, sum2_l,
-    norm_o, gwi, gwo, gm_t, gt_t, gt_o, ggp, rcol, small,
+    part_l, part_h, sum_h, sum_l, acc, grd, gr, gp, dos, ds,
+    norm_o, gwi, gwo, gm_t, gt_t, ggp, rcol, small,
     gain_s, gain_r, col_s, col_r,
     load_sem, ids_ss, ids_rs, mix_ss, mix_rs, raw_ss, raw_rs, a_ss, a_rs, b_ss, b_rs,
     sum_ss, sum_rs, raw2_ss, raw2_rs, c_ss, c_rs, d_ss, d_rs, sum2_ss, sum2_rs,
@@ -110,9 +109,12 @@
         return copy
 
     got_tok = load(tok_h, tok, 0)
-    got_win = load(win_h, win, 1)
-    got_wout = load(wout_h, wout, 2)
-    got_cot = load(cot_h, cot, 3)
+    got_ids = load(ids_h, ids_ref, 1)
+    got_rt = load(rt_h, rt_ref, 2)
+    got_gain = load(gain_h, gain_ref, 3)
+    got_win = load(win_h, win, 4)
+    got_wout = load(wout_h, wout, 5)
+    got_cot = load(cot_h, cot, 6)
 
     barrier = pltpu.get_barrier_semaphore()
     for r in range(1, N):
@@ -120,22 +122,22 @@
     for k in range(1, N):
         pl.semaphore_signal(barrier, inc=1, device_id=(dp, (ex + k) % N), device_id_type=MESH)
     got_tok.wait()
-    tok_t[...] = tok[...].T.reshape(N, head, rows)
-    ids_o[...] = jnp.zeros_like(ids_o)
-    ids_o[0:2, :] = ids_ref[...]
-    pl.semaphore_wait(barrier, 2 * (N - 1))
-    ids_cp = {
-        0: send(ids_o, ids_l, ids_ss.at[0], ids_rs.at[0], high),
-        1: send(ids_o, ids_h, ids_ss.at[1], ids_rs.at[1], low),
-    }
-
-    mix_cp = {}
+    got_ids.wait()
+    ids_own[...] = jnp.zeros_like(ids_own)
+    ids_own[0:2, :] = ids_ref[...]
+
+    ids_cp, mix_cp = {}, {}
     for i in range(NC):
+        c = (xm - i + 4) % 4
+        turned = tok[:, pl.ds(pl.multiple_of(c * part, part), part)].T
+        tok_t[pl.ds(c * tokens4, tokens4)] = turned.reshape(tokens4, head, rows)
+        if i == 0:
+            mix_t[ex] = tok_t[ex]
+            pl.semaphore_wait(barrier, 2 * (N - 1))
         for yy in range(4):
             k = i * 4 + yy
-            to = ((xm - i + 4) % 4) * 4 + (ym + yy) % 4
+            to = c * 4 + (ym + yy) % 4
             if k == 0:
-                mix_t[ex] = tok_t[ex]
                 continue
             mix_cp[k] = pltpu.make_async_remote_copy(
                 src_ref=tok_t.at[to], dst_ref=mix_t.at[ex],
@@ -143,6 +145,9 @@
                 device_id=(dp, to), device_id_type=MESH,
             )
             mix_cp[k].start()
+        if i == 0:
+            ids_cp[0] = send(ids_own, ids_low, ids_ss.at[0], ids_rs.at[0], high)
+            ids_cp[1] = send(ids_own, ids_high, ids_ss.at[1], ids_rs.at[1], low)
 
     label = lax.broadcasted_iota(jnp.int32, (N, rows), 0)
     earlier = (
@@ -178,14 +183,6 @@
             into = arrived if r in HERE else out
             into[r, q] = sent[n * depth : (n + 1) * depth]
 
-    place(ids_o, OWN, po_m, po_t)
-    for c in range(NC):
-        rt4[c] = rt_ref[:, c * part : (c + 1) * part]
-    ids_cp[0].wait_recv()
-    ids_cp[1].wait_recv()
-    place(ids_l, FROM_LOW, pl_m, pl_t)
-    place(ids_h, FROM_HIGH, ph_m, ph_t)
-
     raw_cp, a_cp = {}, {}
 
     def send_mixed(r, i):
@@ -200,11 +197,11 @@
         mixed[c] = mix_t[pl.ds(c * tokens4, tokens4)].reshape(part, rows).T
         raw_cp[0, i] = send(mixed.at[c], raw_l.at[c], raw_ss.at[0, i], raw_rs.at[0, i], high)
         raw_cp[1, i] = send(mixed.at[c], raw_h.at[c], raw_ss.at[1, i], raw_rs.at[1, i], low)
+
+    def pass_on(i):
+        c = (xm + i) % 4
         expand(po_m, mixed[c], OWN, c, xs, xr)
         send_mixed(1, i)
-
-    def pass_on(i):
-        c = (xm + i) % 4
         raw_cp[0, i].wait_recv()
         expand(pl_m, raw_l[c], FROM_LOW, c, xs, xr)
         raw_cp[1, i].wait_recv()
@@ -216,10 +213,19 @@
         mix_chunk(i)
         if i:
             pass_on(i - 1)
+            continue
+        place(ids_own, OWN, po_m, po_t)
+        ids_cp[0].wait_recv()
+        ids_cp[1].wait_recv()
+        place(ids_low, FROM_LOW, pl_m, pl_t)
+        place(ids_high, FROM_HIGH, ph_m, ph_t)
     pass_on(NC - 1)
 
+    got_rt.wait()
     got_win.wait()
     got_wout.wait()
+    for c in range(NC):
+        rt4[c] = rt_ref[:, c * part : (c + 1) * part]
     mine = lax.broadcasted_iota(jnp.int32, (group, N), 1) == dp
     for i in range(NC - 1):
         c = (xm + i) % 4
@@ -273,6 +279,7 @@
     for q in range(NC):
         acc[q] = mixed[q].astype(F32) + dot(po_t[...], stack(yr, OWN, q))
     got_cot.wait()
+    got_gain.wait()
     ggp[...] = jnp.zeros_like(ggp)
 
     def norm_rows(j, carry):
@@ -313,7 +320,7 @@
     for i in range(RUNS):
         lax.fori_loop(i * run // TILE, (i + 1) * run // TILE, norm_rows, 0)
         src = grd.at[:, i * run : (i + 1) * run, :]
-        to_high, to_low = (d.at[:, i * run : (i + 1) * run, :] for d in (raw2_l, raw2_h))
+        to_high, to_low = (d.at[:, i * run : (i + 1) * run, :] for d in (raw_l, raw_h))
         raw2_cp[0, i] = send(src, to_high, raw2_ss.at[0, i], raw2_rs.at[0, i], high)
         raw2_cp[1, i] = send(src, to_low, raw2_ss.at[1, i], raw2_rs.at[1, i], low)
 
@@ -336,16 +343,20 @@
     gn_cp = spread(ggp, small, gain_s, gain_r, gn_ss, gn_rs)
     put_norm = pltpu.make_async_copy(norm_o, no_h, out_sem.at[0])
     put_norm.start()
+    for k in a_cp:
+        a_cp[k].wait_send()
+    for k in sum_cp:
+        sum_cp[k].wait_send()
     for q in range(NC):
-        expand(po_m, grd[q], OWN, q, gs, gr)
+        expand(po_m, grd[q], OWN, q, xs, gr)
     for i in range(RUNS):
         raw2_cp[0, i].wait_recv()
         raw2_cp[1, i].wait_recv()
     for q in range(NC):
-        expand(pl_m, raw2_l[q], FROM_LOW, q, gs, gr)
-        expand(ph_m, raw2_h[q], FROM_HIGH, q, gs, gr)
+        expand(pl_m, raw_l[q], FROM_LOW, q, xs, gr)
+        expand(ph_m, raw_h[q], FROM_HIGH, q, xs, gr)
     for r in AWAY:
-        c_cp[r] = send(gs.at[r], gr.at[r], c_ss.at[r], c_rs.at[r], target(r))
+        c_cp[r] = send(xs.at[r], gr.at[r], c_ss.at[r], c_rs.at[r], target(r))
 
     rcol[...] = jnp.zeros_like(rcol)
     mine_row = lax.broadcasted_iota(jnp.int32, (N, part), 0) == dp
@@ -353,7 +364,7 @@
 
     def send_back(r, i):
         c = (xm + 1 + i) % 4
-        d_cp[r, i] = send(ds.at[r, c], dr.at[r, c], d_ss.at[r, i], d_rs.at[r, i], origin(r))
+        d_cp[r, i] = send(ds.at[r, c], yr.at[r, c], d_ss.at[r, i], d_rs.at[r, i], origin(r))
 
     for g in range(NG):
         at = slice(g * group, (g + 1) * group)
@@ -378,7 +389,7 @@
             ds[4 * g : 4 * g + 4, q] = back
             for r in range(4 * g, 4 * g + 4):
                 if r in HERE:
-                    dr[r, q] = back[r - 4 * g]
+                    yr[r, q] = back[r - 4 * g]
             block = xr[4 * g : 4 * g + 4, q].reshape(group, part).astype(F32)
             rcol[0:1, q * part : (q + 1) * part] += jnp.sum(
                 grad_logit * block, axis=0, keepdims=True
@@ -407,17 +418,17 @@
         c = (xm + 1 + i) % 4
         for r in AWAY:
             d_cp[r, i].wait_recv()
-        part2_l[c] = dot(pl_t[...], stack(dr, FROM_LOW, c)).astype(BF16)
-        sum2_cp[0, i] = send(part2_l.at[c], sum2_h.at[c], sum2_ss.at[0, i], sum2_rs.at[0, i], low)
-        part2_h[c] = dot(ph_t[...], stack(dr, FROM_HIGH, c)).astype(BF16)
-        sum2_cp[1, i] = send(part2_h.at[c], sum2_l.at[c], sum2_ss.at[1, i], sum2_rs.at[1, i], high)
-        acc[c] += dot(po_t[...], stack(dr, OWN, c))
+        part_l[c] = dot(pl_t[...], stack(yr, FROM_LOW, c)).astype(BF16)
+        sum2_cp[0, i] = send(part_l.at[c], sum_h.at[c], sum2_ss.at[0, i], sum2_rs.at[0, i], low)
+        part_h[c] = dot(ph_t[...], stack(yr, FROM_HIGH, c)).astype(BF16)
+        sum2_cp[1, i] = send(part_h.at[c], sum_l.at[c], sum2_ss.at[1, i], sum2_rs.at[1, i], high)
+        acc[c] += dot(po_t[...], stack(yr, OWN, c))
 
     def finish_chunk(i):
         c = (xm + 1 + i) % 4
         sum2_cp[0, i].wait_recv()
         sum2_cp[1, i].wait_recv()
-        total = acc[c] + sum2_h[c].astype(F32) + sum2_l[c].astype(F32)
+        total = acc[c] + sum_h[c].astype(F32) + sum_l[c].astype(F32)
         gm_t[pl.ds(c * tokens4, tokens4)] = total.astype(BF16).T.reshape(tokens4, head, rows)
         for yy in range(4):
             to = c * tokens4 + (ym + yy) % 4
@@ -452,13 +463,17 @@
         for j in range(width // 128):
             gr_ref[e : e + 1, j * 128 : (j + 1) * 128] = small[j : j + 1, :]
 
-    for k in e_cp:
-        e_cp[k].wait_recv()
-    gt_o[...] = gt_t[...].reshape(width, rows).T
-    put_gt = pltpu.make_async_copy(gt_o, gt_h, out_sem.at[3])
+    for i in range(NC):
+        c = (xm + NC - 1 - i) % 4
+        for yy in range(4):
+            if i < NC - 1 or yy:
+                e_cp[i * 4 + yy].wait_recv()
+        turned = gt_t[pl.ds(c * tokens4, tokens4)].reshape(part, rows).T
+        tok[:, pl.ds(pl.multiple_of(c * part, part), part)] = turned
+    put_gt = pltpu.make_async_copy(tok, gt_h, out_sem.at[3])
     put_gt.start()
     for copies in (
-        ids_cp, mix_cp, raw_cp, a_cp, b_cp, sum_cp, raw2_cp, c_cp, d_cp, sum2_cp, e_cp, gn_cp, cl_cp,
+        ids_cp, mix_cp, raw_cp, b_cp, raw2_cp, c_cp, d_cp, sum2_cp, e_cp, gn_cp, cl_cp,
     ):
         for k in copies:
             copies[k].wait_send()
@@ -466,6 +481,23 @@
     put_gwi.wait()
     put_gwo.wait()
     put_gt.wait()
+
+
+def store_kernel(pieces, *refs):
+    count = len(pieces)
+    sems = refs[2 * count]
+    copies = []
+    for k, cut in enumerate(pieces):
+        size = refs[k].shape[0] // cut
+        for i in range(cut):
+            at = slice(i * size, (i + 1) * size)
+            copies.append(
+                pltpu.make_async_copy(refs[k].at[at, :], refs[count + k].at[at, :], sems.at[len(copies)])
+            )
+    for copy in copies:
+        copy.start()
+    for copy in copies:
+        copy.wait()
 
 
 def body(tokens, route_ids, router, norm_gain, w_in, w_out, cotangent):
@@ -478,8 +510,10 @@
     group = 4 * depth
     shape = jax.ShapeDtypeStruct
     vmem = pl.BlockSpec(memory_space=pltpu.VMEM)
-    hbm = pl.BlockSpec(memory_space=pl.ANY)
+    anywhere = pl.BlockSpec(memory_space=pl.ANY)
+    hbm = pl.BlockSpec(memory_space=pltpu.HBM)
     dma = pltpu.SemaphoreType.DMA
+    keep = functools.partial(pltpu.with_memory_space_constraint, memory_space=pltpu.HBM)
     blocks = pltpu.VMEM((N, NC, depth, part), BF16)
     flipped = pltpu.VMEM((N, head, rows), BF16)
     row_block = pltpu.VMEM((rows, width), BF16)
@@ -495,10 +529,13 @@
             shape((width, hidden), BF16),
             shape((hidden, width), BF16),
         ),
-        in_specs=[hbm, vmem, vmem, vmem, hbm, hbm, hbm],
-        out_specs=[hbm, hbm, vmem, vmem, hbm, hbm],
+        in_specs=[hbm] * 7,
+        out_specs=[anywhere, anywhere, vmem, vmem, anywhere, anywhere],
         scratch_shapes=[
             row_block,
+            pltpu.VMEM((2, rows), jnp.int32),
+            pltpu.VMEM((N, width), BF16),
+            pltpu.VMEM((1, width), F32),
             flipped,
             flipped,
             chunks,
@@ -525,20 +562,15 @@
             chunks, chunks, chunks, chunks,
             pltpu.VMEM((NC, rows, part), F32),
             chunks,
-            chunks, chunks,
-            blocks,
             blocks,
             pltpu.VMEM((slots, hidden), BF16),
             pltpu.VMEM((NC, slots, part), BF16),
             blocks,
-            blocks,
-            chunks, chunks, chunks, chunks,
             row_block,
             pltpu.VMEM((width, hidden), BF16),
             pltpu.VMEM((hidden, width), BF16),
             flipped,
             flipped,
-            row_block,
             pltpu.VMEM((8, width), F32),
             pltpu.VMEM((8, width), F32),
             pltpu.VMEM((16, 128), F32),
@@ -546,7 +578,7 @@
             pltpu.VMEM((N, 16, 128), BF16),
             pltpu.VMEM((16, 128), BF16),
             pltpu.VMEM((N, 16, 128), BF16),
-            dma((4,)),
+            dma((7,)),
             dma((2,)), dma((2,)),
             dma((N,)), dma((N,)),
             dma((2, NC)), dma((2, NC)),
@@ -564,17 +596,27 @@
         ],
         name="rank_mixer",
         compiler_params=pltpu.CompilerParams(
-            collective_id=0, has_side_effects=True, vmem_limit_bytes=60 << 20
+            collective_id=0, has_side_effects=True, vmem_limit_bytes=46 << 20
         ),
     )(
-        tokens.reshape(rows, width),
-        route_ids.reshape(rows, 2).T,
-        router.reshape(width, N).T,
-        norm_gain.reshape(1, width),
-        w_in.reshape(width, hidden),
-        w_out.reshape(hidden, width),
-        cotangent.reshape(rows, width),
+        keep(tokens.reshape(rows, width)),
+        keep(route_ids.reshape(rows, 2).T),
+        keep(router.reshape(width, N).T),
+        keep(norm_gain.reshape(1, width)),
+        keep(w_in.reshape(width, hidden)),
+        keep(w_out.reshape(hidden, width)),
+        keep(cotangent.reshape(rows, width)),
     )
+    pieces = (2, 2, 1, 1, 4, 4)
+    out = pl.pallas_call(
+        functools.partial(store_kernel, pieces),
+        out_shape=tuple(shape(v.shape, v.dtype) for v in out),
+        in_specs=[anywhere] * 6,
+        out_specs=[hbm] * 6,
+        scratch_shapes=[dma((sum(pieces),))],
+        name="store",
+        compiler_params=pltpu.CompilerParams(vmem_limit_bytes=1 << 20),
+    )(*out)
     normed_out, grad_tokens, grad_router, grad_gain, grad_w_in, grad_w_out = out
     return (
         normed_out.reshape(rows, 1, width),

time: 242 us -> 229 us (0.946)
  local copies, waits for them, and re-layouts: 9.44 us -> 0 us
  Pallas kernels: 232 us -> 228 us
    unnamed x14 -> x0, local copies, waits for them, and re-layouts: 9.44 us -> none
    pallas_call x1, Pallas kernels: 232 us -> 225 us  [body(): pl.pallas_call(kernel, out_shape=(shape((rows, width), BF16), shape((rows...]
    pallas_call x0 -> x1, Pallas kernels: none -> 2.82 us  [body(): pl.pallas_call(functools.partial(store_kernel, pieces), out_shape=tuple((...]
where the time goes in v3:
time: 229 us
  Pallas kernels  228 us (100%)
    pallas_call x1, Pallas kernels, body(): pl.pallas_call(kernel, out_shape=(shape((rows, width), BF16), shape((rows...  225 us

profile of v3, /device:TPU:1, one launch (start us, length us, event | category | flops | bytes accessed | tf_op | source)
XLA Modules:
  0.0 228.9 jit_solution(4473732202921947620)
XLA Ops:
  0.6 225.2 %rank_mixer.1 = (bf16[256,1536]{1,0:T(8,128)(2,1)S(1)}, bf16[256,1536]{1,0:T(8,128)(2,1)S(1)}, f32[16,1536]{1,0:T(8,128)S(1)}, f32[1,1536]{1,0:T(1,128)S(1)}, bf...) custom-call(bf16[256,1536]{1,0:T(8,128)(2,1)} %bitcast.19, s32[2,256]{1,0:T(2,128)} %bitcast.22, ...), custom_call_target="tpu_custom_call" | custom-call | tf_op jit(solution)/shard_map/rank_mixer/pallas_call | solution.py:522
  225.9 2.8 %store.1 = (bf16[256,1536]{1,0:T(8,128)(2,1)}, bf16[256,1536]{1,0:T(8,128)(2,1)}, f32[16,1536]{1,0:T(8,128)}, f32[1,1536]{1,0:T(1,128)}, bf16[1536,768]{1,0:T(8,128)(2,1)}, /*index=5*/bf16[768,1536]{1,0:T(8,128)(2,1)}) custom-call(bf16[256,1536]{1,0:T(8,128)(2,1)S(1)} %get-tuple-element.18.refs_0_, bf16[256,1536]{1,0:T(8,128)(2,1)S(1)} %get-tuple-element.19.refs_1_, ...), custom_call_target="tpu_custom_call" | custom-call | tf_op jit(solution)/shard_map/store/pallas_call | solution.py:611

commit v4 on v3

--- a/solution.py
+++ b/solution.py
@@ -20,7 +20,6 @@
 NG = 4
 RING = 8
 STEPS = (0, 1, -1, 2, -2, 3, -3, 4)
-BACK = (0, 2, 1, 4, 3, 6, 5, 7)
 HOPS = (0, 0, 0, 0, 0, 0, -1, -1, 1, 1, -2, -2, 2, 2, 3, -3)
 FROM_LOW = (4, 5, 8, 9, 12, 13, 14)
 FROM_HIGH = (2, 3, 6, 7, 10, 11, 15)
@@ -31,10 +30,6 @@
 RUNS = 4
 
 
-def inverse(r):
-    return 2 * BACK[r // 2] + r % 2
-
-
 def dot(a, b):
     return lax.dot_general(a, b, (((1,), (0,)), ((), ())), preferred_element_type=F32)
 
@@ -63,8 +58,8 @@
     tok, ids_ref, rt_ref, gain_ref, tok_t, mix_t, mixed, cot, win, wout, rt4,
     ids_own, ids_low, ids_high, pl_m, ph_m, po_m, pl_t, ph_t, po_t,
     raw_l, raw_h, xs, xr, pre, logit, gate, act, ys, yr,
-    part_l, part_h, sum_h, sum_l, acc, grd, gr, gp, dos, ds,
-    norm_o, gwi, gwo, gm_t, gt_t, ggp, rcol, small,
+    part_l, part_h, sum_h, sum_l, acc, grd, gr, gp, ds, glog,
+    gwi, gwo, gt_t, ggp, rcol, small,
     gain_s, gain_r, col_s, col_r,
     load_sem, ids_ss, ids_rs, mix_ss, mix_rs, raw_ss, raw_rs, a_ss, a_rs, b_ss, b_rs,
     sum_ss, sum_rs, raw2_ss, raw2_rs, c_ss, c_rs, d_ss, d_rs, sum2_ss, sum2_rs,
@@ -110,11 +105,6 @@
 
     got_tok = load(tok_h, tok, 0)
     got_ids = load(ids_h, ids_ref, 1)
-    got_rt = load(rt_h, rt_ref, 2)
-    got_gain = load(gain_h, gain_ref, 3)
-    got_win = load(win_h, win, 4)
-    got_wout = load(wout_h, wout, 5)
-    got_cot = load(cot_h, cot, 6)
 
     barrier = pltpu.get_barrier_semaphore()
     for r in range(1, N):
@@ -123,6 +113,11 @@
         pl.semaphore_signal(barrier, inc=1, device_id=(dp, (ex + k) % N), device_id_type=MESH)
     got_tok.wait()
     got_ids.wait()
+    got_win = load(win_h, win, 4)
+    got_wout = load(wout_h, wout, 5)
+    got_rt = load(rt_h, rt_ref, 2)
+    got_gain = load(gain_h, gain_ref, 3)
+    got_cot = load(cot_h, cot, 6)
     ids_own[...] = jnp.zeros_like(ids_own)
     ids_own[0:2, :] = ids_ref[...]
 
@@ -271,11 +266,19 @@
     sum_cp = {}
     for r in AWAY:
         b_cp[r].wait_recv()
-    for q in range(NC):
-        part_l[q] = dot(pl_t[...], stack(yr, FROM_LOW, q)).astype(BF16)
-        sum_cp[0, q] = send(part_l.at[q], sum_h.at[q], sum_ss.at[0, q], sum_rs.at[0, q], low)
-        part_h[q] = dot(ph_t[...], stack(yr, FROM_HIGH, q)).astype(BF16)
-        sum_cp[1, q] = send(part_h.at[q], sum_l.at[q], sum_ss.at[1, q], sum_rs.at[1, q], high)
+    run = rows // RUNS
+    for i in range(RUNS):
+        at = slice(i * run, (i + 1) * run)
+        for q in range(NC):
+            part_l[q, at] = dot(pl_t[at, :], stack(yr, FROM_LOW, q)).astype(BF16)
+        sum_cp[0, i] = send(
+            part_l.at[:, at, :], sum_h.at[:, at, :], sum_ss.at[0, i], sum_rs.at[0, i], low
+        )
+        for q in range(NC):
+            part_h[q, at] = dot(ph_t[at, :], stack(yr, FROM_HIGH, q)).astype(BF16)
+        sum_cp[1, i] = send(
+            part_h.at[:, at, :], sum_l.at[:, at, :], sum_ss.at[1, i], sum_rs.at[1, i], high
+        )
     for q in range(NC):
         acc[q] = mixed[q].astype(F32) + dot(po_t[...], stack(yr, OWN, q))
     got_cot.wait()
@@ -297,8 +300,8 @@
         grads, m1, m2 = [], 0.0, 0.0
         for q in range(NC):
             gain = gain_ref[0:1, cols[q]]
-            norm_o[at, cols[q]] = (normed[q] * gain).astype(BF16)
             cot_f = cot[at, cols[q]].astype(F32)
+            cot[at, cols[q]] = (normed[q] * gain).astype(BF16)
             ggp[0:1, cols[q]] += jnp.sum(cot_f * normed[q], axis=0, keepdims=True)
             grad = cot_f * gain
             grads.append(grad)
@@ -311,13 +314,10 @@
             grd[q, at, :] = grad.astype(BF16)
         return carry
 
-    for q in range(NC):
-        sum_cp[0, q].wait_recv()
-        sum_cp[1, q].wait_recv()
-
     raw2_cp, c_cp = {}, {}
-    run = rows // RUNS
     for i in range(RUNS):
+        sum_cp[0, i].wait_recv()
+        sum_cp[1, i].wait_recv()
         lax.fori_loop(i * run // TILE, (i + 1) * run // TILE, norm_rows, 0)
         src = grd.at[:, i * run : (i + 1) * run, :]
         to_high, to_low = (d.at[:, i * run : (i + 1) * run, :] for d in (raw_l, raw_h))
@@ -329,20 +329,28 @@
         for j in range(width // 128):
             source[j : j + 1, :] = vector[0:1, j * 128 : (j + 1) * 128]
         target[...] = source[...].astype(BF16)
-        gathered[dp] = target[...]
+        gathered[co, z] = target[...]
         copies = {}
-        for r in range(1, N):
-            copies[r] = pltpu.make_async_remote_copy(
-                src_ref=target, dst_ref=gathered.at[dp],
-                send_sem=send_sems.at[r], recv_sem=recv_sems.at[inverse(r)],
-                device_id=(partner(r), ex), device_id_type=MESH,
+        for k in range(1, RING):
+            copies[k] = send(
+                target, gathered.at[co, z], send_sems.at[k], recv_sems.at[k],
+                ((z + k) % RING) * 2 + co,
             )
-            copies[r].start()
         return copies
 
+    def exchange(copies, gathered, send_sems, recv_sems):
+        for k in range(1, RING):
+            copies[k].wait_recv()
+        copies[0] = send(
+            gathered.at[co], gathered.at[co], send_sems.at[0], recv_sems.at[0],
+            z * 2 + (co + 1) % 2,
+        )
+
     gn_cp = spread(ggp, small, gain_s, gain_r, gn_ss, gn_rs)
-    put_norm = pltpu.make_async_copy(norm_o, no_h, out_sem.at[0])
+    put_norm = pltpu.make_async_copy(cot, no_h, out_sem.at[0])
     put_norm.start()
+    for k in mix_cp:
+        mix_cp[k].wait_send()
     for k in a_cp:
         a_cp[k].wait_send()
     for k in sum_cp:
@@ -378,39 +386,39 @@
             result = ys[4 * g : 4 * g + 4, q].reshape(group, part).astype(F32)
             grad_gate += jnp.sum(grad * result, axis=1, keepdims=True)
             grad_out = (share * grad).astype(BF16)
-            dos[q, at, :] = grad_out
+            gr[4 * g : 4 * g + 4, q] = grad_out.reshape(4, depth, part)
             grad_act += dot_nt(grad_out, wout[:, q * part : (q + 1) * part])
         grad_logit = grad_gate * (1.0 - share)
+        glog[at, :] = grad_logit
         gp[at, :] = (grad_act * pre[at, :]).astype(BF16)
-        for q in range(NC):
-            weights = jnp.sum(jnp.where(mine_row, rt4[q].astype(F32), 0.0), axis=0, keepdims=True)
-            back = dot_nt(gp[at, :], win[q * part : (q + 1) * part, :]) + grad_logit * weights
-            back = back.astype(BF16).reshape(4, depth, part)
-            ds[4 * g : 4 * g + 4, q] = back
+        for i in range(NC):
+            c = (xm + 1 + i) % 4
+            weights = jnp.sum(jnp.where(mine_row, rt4[c].astype(F32), 0.0), axis=0, keepdims=True)
+            back = dot_nt(gp[at, :], win[pl.ds(pl.multiple_of(c * part, part), part), :])
+            back = (back + grad_logit * weights).astype(BF16).reshape(4, depth, part)
+            ds[4 * g : 4 * g + 4, c] = back
             for r in range(4 * g, 4 * g + 4):
                 if r in HERE:
-                    yr[r, q] = back[r - 4 * g]
+                    yr[r, c] = back[r - 4 * g]
+                else:
+                    send_back(r, i)
+
+    for g in range(NG):
+        at = slice(g * group, (g + 1) * group)
+        for q in range(NC):
             block = xr[4 * g : 4 * g + 4, q].reshape(group, part).astype(F32)
             rcol[0:1, q * part : (q + 1) * part] += jnp.sum(
-                grad_logit * block, axis=0, keepdims=True
+                glog[at, :] * block, axis=0, keepdims=True
             )
-        for i in range(2):
-            for r in range(4 * g, 4 * g + 4):
-                if r in AWAY:
-                    send_back(r, i)
-    for i in range(2, NC):
-        for r in AWAY:
-            send_back(r, i)
     cl_cp = spread(rcol, small, col_s, col_r, cl_ss, cl_rs)
-
     for q in range(NC):
         cols = slice(q * part, (q + 1) * part)
         gwi[cols, :] = dot_tn(xr[:, q].reshape(slots, part), gp[...]).astype(BF16)
-        gwo[:, cols] = dot_tn(act[...], dos[q]).astype(BF16)
     put_gwi = pltpu.make_async_copy(gwi, gwi_h, out_sem.at[1])
     put_gwi.start()
-    put_gwo = pltpu.make_async_copy(gwo, gwo_h, out_sem.at[2])
-    put_gwo.start()
+
+    def out_gradient(q):
+        gwo[:, q * part : (q + 1) * part] = dot_tn(act[...], gr[:, q].reshape(slots, part)).astype(BF16)
 
     sum2_cp, e_cp = {}, {}
 
@@ -429,39 +437,50 @@
         sum2_cp[0, i].wait_recv()
         sum2_cp[1, i].wait_recv()
         total = acc[c] + sum_h[c].astype(F32) + sum_l[c].astype(F32)
-        gm_t[pl.ds(c * tokens4, tokens4)] = total.astype(BF16).T.reshape(tokens4, head, rows)
+        tok_t[pl.ds(c * tokens4, tokens4)] = total.astype(BF16).T.reshape(tokens4, head, rows)
         for yy in range(4):
             to = c * tokens4 + (ym + yy) % 4
             if i == NC - 1 and yy == 0:
-                gt_t[ex] = gm_t[ex]
+                gt_t[ex] = tok_t[ex]
                 continue
             k = i * 4 + yy
             e_cp[k] = pltpu.make_async_remote_copy(
-                src_ref=gm_t.at[to], dst_ref=gt_t.at[ex],
+                src_ref=tok_t.at[to], dst_ref=gt_t.at[ex],
                 send_sem=e_ss.at[k], recv_sem=e_rs.at[k],
                 device_id=(dp, to), device_id_type=MESH,
             )
             e_cp[k].start()
 
-    for i in range(NC):
-        sum_back(i)
-        if i:
-            finish_chunk(i - 1)
-    finish_chunk(NC - 1)
-
-    for r in range(1, N):
-        gn_cp[inverse(r)].wait_recv()
-        cl_cp[inverse(r)].wait_recv()
-    total = gain_r[0].astype(F32)
-    for e in range(1, N):
-        total += gain_r[e].astype(F32)
+    sum_back(0)
+    out_gradient(0)
+    out_gradient(1)
+    sum_back(1)
+    finish_chunk(0)
+    out_gradient(2)
+    out_gradient(3)
+    put_gwo = pltpu.make_async_copy(gwo, gwo_h, out_sem.at[2])
+    put_gwo.start()
+    exchange(gn_cp, gain_r, gn_ss, gn_rs)
+    exchange(cl_cp, col_r, cl_ss, cl_rs)
+    sum_back(2)
+    finish_chunk(1)
+
+    gn_cp[0].wait_recv()
+    cl_cp[0].wait_recv()
+    total = 0.0
+    for e in range(N):
+        total += gain_r[e % 2, e // 2].astype(F32)
     small[...] = total
     for j in range(width // 128):
         gg_ref[0:1, j * 128 : (j + 1) * 128] = small[j : j + 1, :]
     for e in range(N):
-        small[...] = col_r[e].astype(F32)
+        small[...] = col_r[e % 2, e // 2].astype(F32)
         for j in range(width // 128):
             gr_ref[e : e + 1, j * 128 : (j + 1) * 128] = small[j : j + 1, :]
+
+    sum_back(3)
+    finish_chunk(2)
+    finish_chunk(3)
 
     for i in range(NC):
         c = (xm + NC - 1 - i) % 4
@@ -473,7 +492,7 @@
     put_gt = pltpu.make_async_copy(tok, gt_h, out_sem.at[3])
     put_gt.start()
     for copies in (
-        ids_cp, mix_cp, raw_cp, b_cp, raw2_cp, c_cp, d_cp, sum2_cp, e_cp, gn_cp, cl_cp,
+        ids_cp, raw_cp, b_cp, raw2_cp, c_cp, d_cp, sum2_cp, e_cp, gn_cp, cl_cp,
     ):
         for k in copies:
             copies[k].wait_send()
@@ -564,27 +583,25 @@
             chunks,
             blocks,
             pltpu.VMEM((slots, hidden), BF16),
-            pltpu.VMEM((NC, slots, part), BF16),
             blocks,
-            row_block,
+            pltpu.VMEM((slots, 1), F32),
             pltpu.VMEM((width, hidden), BF16),
             pltpu.VMEM((hidden, width), BF16),
-            flipped,
             flipped,
             pltpu.VMEM((8, width), F32),
             pltpu.VMEM((8, width), F32),
             pltpu.VMEM((16, 128), F32),
             pltpu.VMEM((16, 128), BF16),
-            pltpu.VMEM((N, 16, 128), BF16),
+            pltpu.VMEM((2, RING, 16, 128), BF16),
             pltpu.VMEM((16, 128), BF16),
-            pltpu.VMEM((N, 16, 128), BF16),
+            pltpu.VMEM((2, RING, 16, 128), BF16),
             dma((7,)),
             dma((2,)), dma((2,)),
             dma((N,)), dma((N,)),
             dma((2, NC)), dma((2, NC)),
             dma((N, NC)), dma((N, NC)),
             dma((N,)), dma((N,)),
-            dma((2, NC)), dma((2, NC)),
+            dma((2, RUNS)), dma((2, RUNS)),
             dma((2, RUNS)), dma((2, RUNS)),
             dma((N,)), dma((N,)),
             dma((N, NC)), dma((N, NC)),

time: 229 us -> 227 us (level)
  Pallas kernels: 228 us -> 225 us
    pallas_call x1, Pallas kernels: 225 us -> 222 us  [body(): pl.pallas_call(kernel, out_shape=(shape((rows, width), BF16), shape((rows...]
where the time goes in v4:
time: 227 us; the launch traced here: 226 us
  Pallas kernels  225 us (99%)
    pallas_call x1, Pallas kernels, body(): pl.pallas_call(kernel, out_shape=(shape((rows, width), BF16), shape((rows...  222 us

profile of v4, /device:TPU:1, one launch (start us, length us, event | category | flops | bytes accessed | tf_op | source)
XLA Modules:
  0.0 225.6 jit_solution(13717094181500779221)
XLA Ops:
  0.6 222.0 %rank_mixer.1 = (bf16[256,1536]{1,0:T(8,128)(2,1)S(1)}, bf16[256,1536]{1,0:T(8,128)(2,1)S(1)}, f32[16,1536]{1,0:T(8,128)S(1)}, f32[1,1536]{1,0:T(1,128)S(1)}, bf...) custom-call(bf16[256,1536]{1,0:T(8,128)(2,1)} %bitcast.19, s32[2,256]{1,0:T(2,128)} %bitcast.22, ...), custom_call_target="tpu_custom_call" | custom-call | tf_op jit(solution)/shard_map/rank_mixer/pallas_call | solution.py:541
  222.6 2.8 %store.1 = (bf16[256,1536]{1,0:T(8,128)(2,1)}, bf16[256,1536]{1,0:T(8,128)(2,1)}, f32[16,1536]{1,0:T(8,128)}, f32[1,1536]{1,0:T(1,128)}, bf16[1536,768]{1,0:T(8,128)(2,1)}, /*index=5*/bf16[768,1536]{1,0:T(8,128)(2,1)}) custom-call(bf16[256,1536]{1,0:T(8,128)(2,1)S(1)} %get-tuple-element.18.refs_0_, bf16[256,1536]{1,0:T(8,128)(2,1)S(1)} %get-tuple-element.19.refs_1_, ...), custom_call_target="tpu_custom_call" | custom-call | tf_op jit(solution)/shard_map/store/pallas_call | solution.py:628

commit v5 on v4

--- a/solution.py
+++ b/solution.py
@@ -57,11 +57,11 @@
     no_h, gt_h, gr_ref, gg_ref, gwi_h, gwo_h,
     tok, ids_ref, rt_ref, gain_ref, tok_t, mix_t, mixed, cot, win, wout, rt4,
     ids_own, ids_low, ids_high, pl_m, ph_m, po_m, pl_t, ph_t, po_t,
-    raw_l, raw_h, xs, xr, pre, logit, gate, act, ys, yr,
+    raw_lt, raw_ht, mix_lt, mix_ht, raw_l, raw_h, xs, xr, pre, logit, gate, act, ys, yr,
     part_l, part_h, sum_h, sum_l, acc, grd, gr, gp, ds, glog,
     gwi, gwo, gt_t, ggp, rcol, small,
     gain_s, gain_r, col_s, col_r,
-    load_sem, ids_ss, ids_rs, mix_ss, mix_rs, raw_ss, raw_rs, a_ss, a_rs, b_ss, b_rs,
+    load_sem, ids_ss, ids_rs, mix_ss, mix_rs, raw_ss, raw_rs, side_ss, side_rs, a_ss, a_rs, b_ss, b_rs,
     sum_ss, sum_rs, raw2_ss, raw2_rs, c_ss, c_rs, d_ss, d_rs, sum2_ss, sum2_rs,
     e_ss, e_rs, gn_ss, gn_rs, cl_ss, cl_rs, out_sem,
 ):
@@ -121,7 +121,7 @@
     ids_own[...] = jnp.zeros_like(ids_own)
     ids_own[0:2, :] = ids_ref[...]
 
-    ids_cp, mix_cp = {}, {}
+    ids_cp, raw_cp, mix_cp = {}, {}, {}
     for i in range(NC):
         c = (xm - i + 4) % 4
         turned = tok[:, pl.ds(pl.multiple_of(c * part, part), part)].T
@@ -129,6 +129,13 @@
         if i == 0:
             mix_t[ex] = tok_t[ex]
             pl.semaphore_wait(barrier, 2 * (N - 1))
+        heads = pl.ds(c * tokens4, tokens4)
+        raw_cp[0, i] = send(
+            tok_t.at[heads], raw_lt.at[heads], raw_ss.at[0, i], raw_rs.at[0, i], high
+        )
+        raw_cp[1, i] = send(
+            tok_t.at[heads], raw_ht.at[heads], raw_ss.at[1, i], raw_rs.at[1, i], low
+        )
         for yy in range(4):
             k = i * 4 + yy
             to = c * 4 + (ym + yy) % 4
@@ -178,43 +185,64 @@
             into = arrived if r in HERE else out
             into[r, q] = sent[n * depth : (n + 1) * depth]
 
-    raw_cp, a_cp = {}, {}
+    a_cp, side_cp = {}, {}
+    sides = ((raw_lt, mix_lt, raw_l), (raw_ht, mix_ht, raw_h))
 
     def send_mixed(r, i):
         c = (xm + i) % 4
         a_cp[r, i] = send(xs.at[r, c], xr.at[r, c], a_ss.at[r, i], a_rs.at[r, i], target(r))
 
-    def mix_chunk(i):
+    def relay(i):
+        c = (xm - i + 4) % 4
+        for n, (whole, gathered, _) in enumerate(sides):
+            raw_cp[n, i].wait_recv()
+            for yy in range(4):
+                k = i * 4 + yy
+                to = c * 4 + (ym + yy) % 4
+                if k == 0:
+                    gathered[ex] = whole[ex]
+                    continue
+                side_cp[n, k] = pltpu.make_async_remote_copy(
+                    src_ref=whole.at[to], dst_ref=gathered.at[ex],
+                    send_sem=side_ss.at[n, k], recv_sem=side_rs.at[n, k],
+                    device_id=(dp, to), device_id_type=MESH,
+                )
+                side_cp[n, k].start()
+
+    def own_chunk(i):
         c = (xm + i) % 4
         for yy in range(4):
             if i * 4 + yy:
                 mix_cp[i * 4 + yy].wait_recv()
         mixed[c] = mix_t[pl.ds(c * tokens4, tokens4)].reshape(part, rows).T
-        raw_cp[0, i] = send(mixed.at[c], raw_l.at[c], raw_ss.at[0, i], raw_rs.at[0, i], high)
-        raw_cp[1, i] = send(mixed.at[c], raw_h.at[c], raw_ss.at[1, i], raw_rs.at[1, i], low)
+        expand(po_m, mixed[c], OWN, c, xs, xr)
+        send_mixed(1, i)
 
     def pass_on(i):
         c = (xm + i) % 4
-        expand(po_m, mixed[c], OWN, c, xs, xr)
-        send_mixed(1, i)
-        raw_cp[0, i].wait_recv()
-        expand(pl_m, raw_l[c], FROM_LOW, c, xs, xr)
-        raw_cp[1, i].wait_recv()
-        expand(ph_m, raw_h[c], FROM_HIGH, c, xs, xr)
+        for n, (_, gathered, plain) in enumerate(sides):
+            for yy in range(4):
+                if i * 4 + yy:
+                    side_cp[n, i * 4 + yy].wait_recv()
+            plain[c] = gathered[pl.ds(c * tokens4, tokens4)].reshape(part, rows).T
+            if n == 0:
+                expand(pl_m, plain[c], FROM_LOW, c, xs, xr)
+            else:
+                expand(ph_m, plain[c], FROM_HIGH, c, xs, xr)
         for r in AWAY[1:]:
             send_mixed(r, i)
 
+    place(ids_own, OWN, po_m, po_t)
+    ids_cp[0].wait_recv()
+    ids_cp[1].wait_recv()
+    place(ids_low, FROM_LOW, pl_m, pl_t)
+    place(ids_high, FROM_HIGH, ph_m, ph_t)
+    relay(0)
     for i in range(NC):
-        mix_chunk(i)
-        if i:
-            pass_on(i - 1)
-            continue
-        place(ids_own, OWN, po_m, po_t)
-        ids_cp[0].wait_recv()
-        ids_cp[1].wait_recv()
-        place(ids_low, FROM_LOW, pl_m, pl_t)
-        place(ids_high, FROM_HIGH, ph_m, ph_t)
-    pass_on(NC - 1)
+        own_chunk(i)
+        if i + 1 < NC:
+            relay(i + 1)
+        pass_on(i)
 
     got_rt.wait()
     got_win.wait()
@@ -349,8 +377,9 @@
     gn_cp = spread(ggp, small, gain_s, gain_r, gn_ss, gn_rs)
     put_norm = pltpu.make_async_copy(cot, no_h, out_sem.at[0])
     put_norm.start()
-    for k in mix_cp:
-        mix_cp[k].wait_send()
+    for copies in (mix_cp, raw_cp):
+        for k in copies:
+            copies[k].wait_send()
     for k in a_cp:
         a_cp[k].wait_send()
     for k in sum_cp:
@@ -492,7 +521,7 @@
     put_gt = pltpu.make_async_copy(tok, gt_h, out_sem.at[3])
     put_gt.start()
     for copies in (
-        ids_cp, raw_cp, b_cp, raw2_cp, c_cp, d_cp, sum2_cp, e_cp, gn_cp, cl_cp,
+        ids_cp, side_cp, b_cp, raw2_cp, c_cp, d_cp, sum2_cp, e_cp, gn_cp, cl_cp,
     ):
         for k in copies:
             copies[k].wait_send()
@@ -569,6 +598,7 @@
             pltpu.VMEM((rows, 7 * depth), BF16),
             pltpu.VMEM((rows, 7 * depth), BF16),
             pltpu.VMEM((rows, 2 * depth), BF16),
+            flipped, flipped, flipped, flipped,
             chunks, chunks,
             blocks,
             blocks,
@@ -599,6 +629,7 @@
             dma((2,)), dma((2,)),
             dma((N,)), dma((N,)),
             dma((2, NC)), dma((2, NC)),
+            dma((2, N)), dma((2, N)),
             dma((N, NC)), dma((N, NC)),
             dma((N,)), dma((N,)),
             dma((2, RUNS)), dma((2, RUNS)),

time: 227 us -> 221 us (0.974)
  Pallas kernels: 225 us -> 220 us
    pallas_call x1, Pallas kernels: 222 us -> 218 us  [body(): pl.pallas_call(kernel, out_shape=(shape((rows, width), BF16), shape((rows...]
where the time goes in v5:
time: 221 us
  Pallas kernels  220 us (100%)
    pallas_call x1, Pallas kernels, body(): pl.pallas_call(kernel, out_shape=(shape((rows, width), BF16), shape((rows...  218 us

profile of v5, /device:TPU:1, one launch (start us, length us, event | category | flops | bytes accessed | tf_op | source)
XLA Modules:
  0.0 221.2 jit_solution(17188370619777654445)
XLA Ops:
  0.6 217.5 %rank_mixer.1 = (bf16[256,1536]{1,0:T(8,128)(2,1)S(1)}, bf16[256,1536]{1,0:T(8,128)(2,1)S(1)}, f32[16,1536]{1,0:T(8,128)S(1)}, f32[1,1536]{1,0:T(1,128)S(1)}, bf...) custom-call(bf16[256,1536]{1,0:T(8,128)(2,1)} %bitcast.19, s32[2,256]{1,0:T(2,128)} %bitcast.22, ...), custom_call_target="tpu_custom_call" | custom-call | tf_op jit(solution)/shard_map/rank_mixer/pallas_call | solution.py:570
  218.2 2.8 %store.1 = (bf16[256,1536]{1,0:T(8,128)(2,1)}, bf16[256,1536]{1,0:T(8,128)(2,1)}, f32[16,1536]{1,0:T(8,128)}, f32[1,1536]{1,0:T(1,128)}, bf16[1536,768]{1,0:T(8,128)(2,1)}, /*index=5*/bf16[768,1536]{1,0:T(8,128)(2,1)}) custom-call(bf16[256,1536]{1,0:T(8,128)(2,1)S(1)} %get-tuple-element.18.refs_0_, bf16[256,1536]{1,0:T(8,128)(2,1)S(1)} %get-tuple-element.19.refs_1_, ...), custom_call_target="tpu_custom_call" | custom-call | tf_op jit(solution)/shard_map/store/pallas_call | solution.py:659

commit v6 on v5

--- a/solution.py
+++ b/solution.py
@@ -179,8 +179,9 @@
     def stack(blocks, members, q):
         return jnp.concatenate([blocks[r, q] for r in members], axis=0)
 
-    def expand(matrix, values, members, q, out, arrived):
-        sent = dot(matrix[...], values).astype(BF16)
+    def expand(matrix, values, members, q, out, arrived, first=0):
+        at = slice(first * depth, (first + len(members)) * depth)
+        sent = dot(matrix[at, :], values).astype(BF16)
         for n, r in enumerate(members):
             into = arrived if r in HERE else out
             into[r, q] = sent[n * depth : (n + 1) * depth]
@@ -386,14 +387,22 @@
         sum_cp[k].wait_send()
     for q in range(NC):
         expand(po_m, grd[q], OWN, q, xs, gr)
-    for i in range(RUNS):
-        raw2_cp[0, i].wait_recv()
-        raw2_cp[1, i].wait_recv()
-    for q in range(NC):
-        expand(pl_m, raw_l[q], FROM_LOW, q, xs, gr)
-        expand(ph_m, raw_h[q], FROM_HIGH, q, xs, gr)
-    for r in AWAY:
+    def send_gradient(r):
         c_cp[r] = send(xs.at[r], gr.at[r], c_ss.at[r], c_rs.at[r], target(r))
+
+    send_gradient(1)
+    for first, last in ((0, 4), (4, 7)):
+        for n, (matrix, values, members) in enumerate(
+            ((pl_m, raw_l, FROM_LOW), (ph_m, raw_h, FROM_HIGH))
+        ):
+            if first == 0:
+                for i in range(RUNS):
+                    raw2_cp[n, i].wait_recv()
+            for q in range(NC):
+                expand(matrix, values[q], members[first:last], q, xs, gr, first)
+            for r in members[first:last]:
+                if r in AWAY:
+                    send_gradient(r)
 
     rcol[...] = jnp.zeros_like(rcol)
     mine_row = lax.broadcasted_iota(jnp.int32, (N, part), 0) == dp
@@ -494,6 +503,8 @@
     sum_back(2)
     finish_chunk(1)
 
+    sum_back(3)
+
     gn_cp[0].wait_recv()
     cl_cp[0].wait_recv()
     total = 0.0
@@ -507,7 +518,6 @@
         for j in range(width // 128):
             gr_ref[e : e + 1, j * 128 : (j + 1) * 128] = small[j : j + 1, :]
 
-    sum_back(3)
     finish_chunk(2)
     finish_chunk(3)
 

time: 221 us -> 222 us (level)
  no operation moved by 1% of the time
where the time goes in v6:
time: 222 us; the launch traced here: 221 us
  Pallas kernels  221 us (100%)
    pallas_call x1, Pallas kernels, body(): pl.pallas_call(kernel, out_shape=(shape((rows, width), BF16), shape((rows...  218 us

profile of v6, /device:TPU:1, one launch (start us, length us, event | category | flops | bytes accessed | tf_op | source)
XLA Modules:
  0.0 221.4 jit_solution(7545704337595168157)
XLA Ops:
  0.6 217.8 %rank_mixer.1 = (bf16[256,1536]{1,0:T(8,128)(2,1)S(1)}, bf16[256,1536]{1,0:T(8,128)(2,1)S(1)}, f32[16,1536]{1,0:T(8,128)S(1)}, f32[1,1536]{1,0:T(1,128)S(1)}, bf...) custom-call(bf16[256,1536]{1,0:T(8,128)(2,1)} %bitcast.19, s32[2,256]{1,0:T(2,128)} %bitcast.22, ...), custom_call_target="tpu_custom_call" | custom-call | tf_op jit(solution)/shard_map/rank_mixer/pallas_call | solution.py:580
  218.4 2.8 %store.1 = (bf16[256,1536]{1,0:T(8,128)(2,1)}, bf16[256,1536]{1,0:T(8,128)(2,1)}, f32[16,1536]{1,0:T(8,128)}, f32[1,1536]{1,0:T(1,128)}, bf16[1536,768]{1,0:T(8,128)(2,1)}, /*index=5*/bf16[768,1536]{1,0:T(8,128)(2,1)}) custom-call(bf16[256,1536]{1,0:T(8,128)(2,1)S(1)} %get-tuple-element.18.refs_0_, bf16[256,1536]{1,0:T(8,128)(2,1)S(1)} %get-tuple-element.19.refs_1_, ...), custom_call_target="tpu_custom_call" | custom-call | tf_op jit(solution)/shard_map/store/pallas_call | solution.py:669

commit v7 on v6

--- a/solution.py
+++ b/solution.py
@@ -63,7 +63,7 @@
     gain_s, gain_r, col_s, col_r,
     load_sem, ids_ss, ids_rs, mix_ss, mix_rs, raw_ss, raw_rs, side_ss, side_rs, a_ss, a_rs, b_ss, b_rs,
     sum_ss, sum_rs, raw2_ss, raw2_rs, c_ss, c_rs, d_ss, d_rs, sum2_ss, sum2_rs,
-    e_ss, e_rs, gn_ss, gn_rs, cl_ss, cl_rs, out_sem,
+    e_ss, e_rs, gn_ss, gn_rs, cl_ss, cl_rs, out_sem, put_sem,
 ):
     rows, width = tok.shape
     head = width // N
@@ -498,6 +498,9 @@
     out_gradient(3)
     put_gwo = pltpu.make_async_copy(gwo, gwo_h, out_sem.at[2])
     put_gwo.start()
+    for copies in (ids_cp, side_cp, b_cp, raw2_cp, c_cp):
+        for k in copies:
+            copies[k].wait_send()
     exchange(gn_cp, gain_r, gn_ss, gn_rs)
     exchange(cl_cp, col_r, cl_ss, cl_rs)
     sum_back(2)
@@ -519,26 +522,37 @@
             gr_ref[e : e + 1, j * 128 : (j + 1) * 128] = small[j : j + 1, :]
 
     finish_chunk(2)
-    finish_chunk(3)
-
-    for i in range(NC):
+    for copies in (d_cp, gn_cp, cl_cp):
+        for k in copies:
+            copies[k].wait_send()
+    put_gt = []
+
+    def place_tokens(i):
         c = (xm + NC - 1 - i) % 4
         for yy in range(4):
             if i < NC - 1 or yy:
                 e_cp[i * 4 + yy].wait_recv()
-        turned = gt_t[pl.ds(c * tokens4, tokens4)].reshape(part, rows).T
-        tok[:, pl.ds(pl.multiple_of(c * part, part), part)] = turned
-    put_gt = pltpu.make_async_copy(tok, gt_h, out_sem.at[3])
-    put_gt.start()
-    for copies in (
-        ids_cp, side_cp, b_cp, raw2_cp, c_cp, d_cp, sum2_cp, e_cp, gn_cp, cl_cp,
-    ):
-        for k in copies:
-            copies[k].wait_send()
+        cols = pl.ds(pl.multiple_of(c * part, part), part)
+        tok[:, cols] = gt_t[pl.ds(c * tokens4, tokens4)].reshape(part, rows).T
+        put_gt.append(
+            pltpu.make_async_copy(tok.at[:, cols], gt_h.at[:, cols], put_sem.at[i])
+        )
+        put_gt[i].start()
+
+    place_tokens(0)
+    place_tokens(1)
     put_norm.wait()
     put_gwi.wait()
     put_gwo.wait()
-    put_gt.wait()
+    finish_chunk(3)
+    place_tokens(2)
+    place_tokens(3)
+
+    for copies in (sum2_cp, e_cp):
+        for k in copies:
+            copies[k].wait_send()
+    for put in put_gt:
+        put.wait()
 
 
 def store_kernel(pieces, *refs):
@@ -650,7 +664,8 @@
             dma((N,)), dma((N,)),
             dma((N,)), dma((N,)),
             dma((N,)), dma((N,)),
-            dma((4,)),
+            dma((3,)),
+            dma((NC,)),
         ],
         name="rank_mixer",
         compiler_params=pltpu.CompilerParams(

time: 222 us -> 222 us (level)
  no operation moved by 1% of the time
where the time goes in v7:
time: 222 us
  Pallas kernels  221 us (100%)
    pallas_call x1, Pallas kernels, body(): pl.pallas_call(kernel, out_shape=(shape((rows, width), BF16), shape((rows...  218 us

profile of v7, /device:TPU:1, one launch (start us, length us, event | category | flops | bytes accessed | tf_op | source)
XLA Modules:
  0.0 221.9 jit_solution(10580854568272222679)
XLA Ops:
  0.6 218.3 %rank_mixer.1 = (bf16[256,1536]{1,0:T(8,128)(2,1)S(1)}, bf16[256,1536]{1,0:T(8,128)(2,1)S(1)}, f32[16,1536]{1,0:T(8,128)S(1)}, f32[1,1536]{1,0:T(1,128)S(1)}, bf...) custom-call(bf16[256,1536]{1,0:T(8,128)(2,1)} %bitcast.19, s32[2,256]{1,0:T(2,128)} %bitcast.22, ...), custom_call_target="tpu_custom_call" | custom-call | tf_op jit(solution)/shard_map/rank_mixer/pallas_call | solution.py:594
  218.9 2.8 %store.1 = (bf16[256,1536]{1,0:T(8,128)(2,1)}, bf16[256,1536]{1,0:T(8,128)(2,1)}, f32[16,1536]{1,0:T(8,128)}, f32[1,1536]{1,0:T(1,128)}, bf16[1536,768]{1,0:T(8,128)(2,1)}, /*index=5*/bf16[768,1536]{1,0:T(8,128)(2,1)}) custom-call(bf16[256,1536]{1,0:T(8,128)(2,1)S(1)} %get-tuple-element.18.refs_0_, bf16[256,1536]{1,0:T(8,128)(2,1)S(1)} %get-tuple-element.19.refs_1_, ...), custom_call_target="tpu_custom_call" | custom-call | tf_op jit(solution)/shard_map/store/pallas_call | solution.py:684

commit v8 on v7

--- a/solution.py
+++ b/solution.py
@@ -27,7 +27,7 @@
 HERE = (0, 2, 4)
 AWAY = tuple(r for r in range(N) if r not in HERE)
 TILE = 32
-RUNS = 4
+RUNS = 8
 
 
 def dot(a, b):
@@ -230,7 +230,7 @@
                 expand(pl_m, plain[c], FROM_LOW, c, xs, xr)
             else:
                 expand(ph_m, plain[c], FROM_HIGH, c, xs, xr)
-        for r in AWAY[1:]:
+        for r in AWAY[:0:-1]:
             send_mixed(r, i)
 
     place(ids_own, OWN, po_m, po_t)
@@ -268,7 +268,7 @@
                 logit[at, :] += more_logit
     b_cp = {}
     c = (xm + NC - 1) % 4
-    for g in range(NG):
+    for g in (0, 3, 2, 1):
         at = slice(g * group, (g + 1) * group)
         for r in range(4 * g, 4 * g + 4):
             if r in AWAY:
@@ -391,11 +391,11 @@
         c_cp[r] = send(xs.at[r], gr.at[r], c_ss.at[r], c_rs.at[r], target(r))
 
     send_gradient(1)
-    for first, last in ((0, 4), (4, 7)):
+    for first, last in ((4, 7), (0, 4)):
         for n, (matrix, values, members) in enumerate(
             ((pl_m, raw_l, FROM_LOW), (ph_m, raw_h, FROM_HIGH))
         ):
-            if first == 0:
+            if first:
                 for i in range(RUNS):
                     raw2_cp[n, i].wait_recv()
             for q in range(NC):
@@ -412,7 +412,7 @@
         c = (xm + 1 + i) % 4
         d_cp[r, i] = send(ds.at[r, c], yr.at[r, c], d_ss.at[r, i], d_rs.at[r, i], origin(r))
 
-    for g in range(NG):
+    for g in (0, 3, 2, 1):
         at = slice(g * group, (g + 1) * group)
         for r in range(4 * g, 4 * g + 4):
             if r in AWAY:

time: 222 us -> 219 us (0.986)
  Pallas kernels: 221 us -> 218 us
    pallas_call x1, Pallas kernels: 218 us -> 216 us  [body(): pl.pallas_call(kernel, out_shape=(shape((rows, width), BF16), shape((rows...]
where the time goes in v8:
time: 219 us
  Pallas kernels  218 us (100%)
    pallas_call x1, Pallas kernels, body(): pl.pallas_call(kernel, out_shape=(shape((rows, width), BF16), shape((rows...  216 us

profile of v8, /device:TPU:1, one launch (start us, length us, event | category | flops | bytes accessed | tf_op | source)
XLA Modules:
  0.0 219.3 jit_solution(10332126373926913444)
XLA Ops:
  0.6 215.7 %rank_mixer.1 = (bf16[256,1536]{1,0:T(8,128)(2,1)S(1)}, bf16[256,1536]{1,0:T(8,128)(2,1)S(1)}, f32[16,1536]{1,0:T(8,128)S(1)}, f32[1,1536]{1,0:T(1,128)S(1)}, bf...) custom-call(bf16[256,1536]{1,0:T(8,128)(2,1)} %bitcast.19, s32[2,256]{1,0:T(2,128)} %bitcast.22, ...), custom_call_target="tpu_custom_call" | custom-call | tf_op jit(solution)/shard_map/rank_mixer/pallas_call | solution.py:594
  216.3 2.8 %store.1 = (bf16[256,1536]{1,0:T(8,128)(2,1)}, bf16[256,1536]{1,0:T(8,128)(2,1)}, f32[16,1536]{1,0:T(8,128)}, f32[1,1536]{1,0:T(1,128)}, bf16[1536,768]{1,0:T(8,128)(2,1)}, /*index=5*/bf16[768,1536]{1,0:T(8,128)(2,1)}) custom-call(bf16[256,1536]{1,0:T(8,128)(2,1)S(1)} %get-tuple-element.18.refs_0_, bf16[256,1536]{1,0:T(8,128)(2,1)S(1)} %get-tuple-element.19.refs_1_, ...), custom_call_target="tpu_custom_call" | custom-call | tf_op jit(solution)/shard_map/store/pallas_call | solution.py:684
